TPU v7x, 512 devices: a whole 4x4x16 slice. The times are simulated.
512 devices in a mesh: row: 8 (over x_hi, y), pair: 64 (over z, x_lo, core).
Axes of the slice: x: 4 (x_hi: 2, x_lo: 2; x = x_hi * 2 + x_lo), y: 4, z: 16, core: 2. Of those that a mesh axis runs over, the one named last changes fastest.
Arguments:
- panel: float32 [16384, 16384], P('row', 'pair'), may hold values from -51 to 51
- slot_block: int32 [128], replicated, may hold values from 0 to 127, each once
Outputs:
- rotated: float32 [16384, 16384], P('row', 'pair')
Inputs may be any that keep to these rules, and one draw needn't show every extreme that they name: `slot_block`: each block number appears once.
All inputs are finite; a program needn't handle non-finite values.
Results may differ from a plain program's by a relative error of at most 0.0003.
Values sent between devices are 32-bit elements; how exact they have to be, the bound alone decides.
No kernel may reach another device: no remote copies, remote signals or barrier semaphores. Data moves between devices by JAX's collectives and lax.ppermute only.
A program may use at most 64 MiB of HBM per device.

v0:
```python
import jax
import jax.numpy as jnp
from jax import lax
from jax.sharding import PartitionSpec as P

STEPS = 2
NS_ITERS = 3


precise = lax.Precision.HIGHEST


def copy_for_each(shard, axis):
    copies = jnp.broadcast_to(shard, (lax.axis_size(axis), *shard.shape))
    return lax.all_to_all(copies, axis, split_axis=0, concat_axis=0, tiled=True)


def of_everyone(shard, axis):
    everything = copy_for_each(shard, axis)
    return jnp.sum(everything, axis=0)


def passed_along(value, axis, steps):
    count = lax.axis_size(axis)
    initial, last = (max(0, -steps), min(count, count - steps))
    return lax.ppermute(value, axis, [(source, source + steps) for source in range(initial, last)])


def inverse_root(matrix):
    identity = jnp.eye(matrix.shape[0], dtype=matrix.dtype)
    approx = matrix
    root_inv = identity
    for sweep in range(NS_ITERS):
        factor = 1.5 * identity - 0.5 * jnp.dot(root_inv, approx, precision=precise)
        approx = jnp.dot(approx, factor, precision=precise)
        root_inv = jnp.dot(factor, root_inv, precision=precise)
    return root_inv / jnp.sqrt(5.0)


def couple(cross):
    identity = jnp.eye(cross.shape[0], dtype=cross.dtype)
    coupling = cross * (2.0 / jnp.sqrt(jnp.sum(cross * cross) + 1e-06))
    left = (identity + jnp.dot(coupling, coupling.T, precision=precise)) / 5.0
    right = (identity + jnp.dot(coupling.T, coupling, precision=precise)) / 5.0
    return (coupling, left, right)


def inner_rows(first, second):
    return lax.dot_general(first, second, (((0,), (0,)), ((), ())), precision=precise)


def move_slots(uppers, lowers):
    new_uppers = jnp.concatenate([uppers[0:1], lowers[0:1], uppers[1:-1]], axis=0)
    new_lowers = jnp.concatenate([lowers[1:], uppers[-1:]], axis=0)
    return (new_uppers, new_lowers)


def jacobi_step(upper, lower, upper_ids, lower_ids, position, pairs):
    matching = jnp.arange(pairs) == position
    upper_id = jnp.sum(jnp.where(matching, upper_ids, 0))
    lower_id = jnp.sum(jnp.where(matching, lower_ids, 0))
    order_flag = upper_id < lower_id
    first = jnp.where(order_flag, upper, lower)
    second = jnp.where(order_flag, lower, upper)
    cross = of_everyone(inner_rows(first, second), "row")
    coupling, left, right = couple(cross)
    left_inverse = inverse_root(left)
    right_inverse = inverse_root(right)
    new_first = jnp.dot(
        first + jnp.dot(second, coupling.T, precision=precise), left_inverse, precision=precise
    )
    new_second = jnp.dot(
        second - jnp.dot(first, coupling, precision=precise), right_inverse, precision=precise
    )
    new_upper = jnp.where(order_flag, new_first, new_second)
    new_lower = jnp.where(order_flag, new_second, new_first)
    carried = jnp.where(position == 0, new_lower, new_upper)
    from_left = passed_along(carried, "pair", 1)
    from_right = passed_along(new_lower, "pair", -1)
    moved_upper = jnp.where(position == 0, new_upper, from_left)
    moved_lower = jnp.where(position == pairs - 1, new_upper, from_right)
    return (moved_upper, moved_lower)


def per_device(panel, slot_block):
    width = panel.shape[1] // 2
    pairs = lax.axis_size("pair")
    position = lax.axis_index("pair")
    upper = panel[:, :width]
    lower = panel[:, width:]
    upper_ids = slot_block[:pairs]
    lower_ids = slot_block[pairs:]
    for step in range(STEPS):
        upper, lower = jacobi_step(upper, lower, upper_ids, lower_ids, position, pairs)
        upper_ids, lower_ids = move_slots(upper_ids, lower_ids)
    return jnp.concatenate([upper, lower], axis=1)


def solution(mesh):
    in_specs = (P("row", "pair"), P())
    out_specs = P("row", "pair")
    return jax.shard_map(
        per_device, mesh=mesh, in_specs=in_specs, out_specs=out_specs, check_vma=False
    )
```

profile of v0, /device:TPU:1, one launch (start us, length us, event | category | flops | bytes accessed | tf_op | source)
XLA Modules:
  0.0 119.7 jit_solution(15180968800029673013)
XLA Ops:
  0.0 1.5 %select_reduce_fusion = (s32[]{:T(128)}, s32[]{:T(128)}) fusion(s32[128]{0:T(128)} %param.3, s32[]{:T(128)S(6)} %axis_index.12), kind=kLoop, calls=%fused_computation.82 | loop fusion | flops 318 | bytes 524 | tf_op jit(solution)/shard_map/reduce_sum | solution.py:61
  2.9 1.7 %slice_select_fusion.1 = (f32[2048,128]{1,0:T(8,128)S(1)}, f32[2048,128]{1,0:T(8,128)S(1)}) fusion(f32[2048,256]{1,0:T(8,128)} %param.2, pred[]{:T(512)S(6)} %lt.7), kind=kLoop, calls=%fused_computation.42 | loop fusion | flops 524288 | bytes 4194305 | tf_op jit(solution)/shard_map/jit(_where)/select_n | solution.py:63
  4.5 1.8 %fusion.39 = f32[128,128]{1,0:T(8,128)S(1)} fusion(f32[2048,128]{1,0:T(8,128)S(1)} %get-tuple-element.15, f32[2048,128]{1,0:T(8,128)S(1)} %get-tuple-element.16), kind=kOutput, calls=%fused_computation.86 | convolution fusion | flops 402653184 | bytes 2162688 | tf_op jit(solution)/shard_map/dot_general | solution.py:49
  7.2 7.5 %all-to-all-start = ((f32[8,128,128]{2,1,0:T(8,128)}), f32[8,128,128]{2,1,0:T(8,128)S(1)}, u32[]{:S(2)}, u32[]{:S(2)}) async-start(f32[8,128,128]{2,1,0:T(8,128)} %broadcast_in_dim.14), calls=%async_computation | async-start | bytes 1048576 | tf_op jit(solution)/shard_map/all_to_all | solution.py:15
  14.7 8.8 %all-to-all-done = f32[8,128,128]{2,1,0:T(8,128)S(1)} async-done(((f32[8,128,128]{2,1,0:T(8,128)}), f32[8,128,128]{2,1,0:T(8,128)S(1)}, u32[]{:S(2)}, u32[]{:S(2)}) %all-to-all-start) | async-done | bytes 524320 | tf_op jit(solution)/shard_map/all_to_all | solution.py:15
  27.8 1.0 convolution_subtract_fusion.1
  28.8 1.0 convolution_add_fusion.1
  30.7 1.0 fusion.43
  31.7 1.9 %broadcast_select_fusion.11 = (f32[2048,128]{1,0:T(8,128)}, f32[2048,128]{1,0:T(8,128)S(1)}, f32[2048,128]{1,0:T(8,128)S(1)}) fusion(pred[]{:T(512)S(6)} %eq.72, f32[2048,128]{1,0:T(8,128)S(1)} %fusion.43, pred[]{:T(512)S(6)} %lt.7, f32[2048,128]{1,0:T(8,128)S(1)} %convolution_subtract_fusion.1, f32[128,128]{1,0:T(8,128)S(1)} %convolution_multiply_fusion.8), kind=kOutput, calls=%fused_computation.54 | convolution fusion | flops 403439616 | bytes 5308418 | tf_op jit(solution)/shard_map/dot_general | solution.py:72
  33.6 5.3 %collective-permute-start = (f32[2048,128]{1,0:T(8,128)}, f32[2048,128]{1,0:T(8,128)S(1)}, u32[]{:S(2)}, u32[]{:S(2)}) collective-permute-start(f32[2048,128]{1,0:T(8,128)} %get-tuple-element.10), channel_id=1, source_target_pairs={{0,1},{1,2},{2,3},{3,4},{4,5},{5,6},{6,7},{7,8},{8,9},{9,10},{10,1... | collective-permute-start | bytes 3145736 | tf_op jit(solution)/shard_map/ppermute | solution.py:26
  38.9 1.9 %collective-permute-start.1 = (f32[2048,128]{1,0:T(8,128)S(1)}, f32[2048,128]{1,0:T(8,128)}, u32[]{:S(2)}, u32[]{:S(2)}) collective-permute-start(f32[2048,128]{1,0:T(8,128)S(1)} %get-tuple-element.11), channel_id=1, source_target_pairs={{1,0},{2,1},{3,2},{4,3},{5,4},{6,5},{7,6},{8,7},{9,8},{10,9},{11,1... | collective-permute-start | bytes 3145736 | tf_op jit(solution)/shard_map/ppermute | solution.py:26
  41.7 2.6 %fusion.36 = (s32[]{:T(128)}, s32[]{:T(128)}) fusion(s32[62]{0:T(128)S(1)} %slice.34, s32[1]{0:T(128)} %get-tuple-element.20, s32[1]{0:T(128)} %get-tuple-element.21, s32[]{:T(128)S(6)} %axis_index.12, s32[1]{0:T(128)} %get-tuple-element.19, s32[63]{0:T(128)S(1)} %slice.35), kind=kLoop, calls=%fused_computation.79 | loop fusion | flops 510 | bytes 524 | tf_op jit(solution)/shard_map/reduce_sum | solution.py:60
  45.5 19.5 %collective-permute-done = f32[2048,128]{1,0:T(8,128)S(1)} collective-permute-done((f32[2048,128]{1,0:T(8,128)}, f32[2048,128]{1,0:T(8,128)S(1)}, u32[]{:S(2)}, u32[]{:S(2)}) %collective-permute-start) | collective-permute-done | bytes 1048608 | tf_op jit(solution)/shard_map/ppermute | solution.py:26
  66.0 1.7 %broadcast_select_fusion.7 = (f32[2048,128]{1,0:T(8,128)S(1)}, f32[2048,128]{1,0:T(8,128)S(1)}) fusion(pred[]{:T(512)S(6)} %lt.6, f32[2048,128]{1,0:T(8,128)S(1)} %get-tuple-element.12, f32[2048,128]{1,0:T(8,128)} %copy-done, pred[]{:T(512)S(6)} %eq.72, f32[2048,128]{1,0:T(8,128)} %collective-permute-done.1, pred[]{:T(512)S(6)} %eq.76), kind=kLoop, calls=%fused_computation.50 | loop fusion | flops 1048576 | bytes 5242883 | tf_op jit(solution)/shard_map/jit(_where)/select_n | solution.py:63
  67.7 1.8 %fusion.47 = f32[128,128]{1,0:T(8,128)S(1)} fusion(f32[2048,128]{1,0:T(8,128)S(1)} %get-tuple-element.13, f32[2048,128]{1,0:T(8,128)S(1)} %get-tuple-element.14), kind=kOutput, calls=%fused_computation.94 | convolution fusion | flops 402653184 | bytes 2162688 | tf_op jit(solution)/shard_map/dot_general | solution.py:49
  69.6 12.4 %all_to_all.10 = f32[8,128,128]{2,1,0:T(8,128)S(1)} all-to-all(f32[8,128,128]{2,1,0:T(8,128)S(1)} %broadcast_in_dim.15), channel_id=1, replica_groups=mesh['row'=8,'pair'=64] {'row'}, dimensions={0} | all-to-all | bytes 1048576 | tf_op jit(solution)/shard_map/all_to_all | solution.py:15
  86.3 1.0 convolution_subtract_fusion
  87.3 1.0 convolution_add_fusion
  89.1 1.0 fusion.51
  90.1 1.0 broadcast_select_fusion.9
  91.1 5.1 %collective-permute-start.2 = (f32[2048,128]{1,0:T(8,128)S(1)}, f32[2048,128]{1,0:T(8,128)S(1)}, u32[]{:S(2)}, u32[]{:S(2)}) collective-permute-start(f32[2048,128]{1,0:T(8,128)S(1)} %get-tuple-element.7), channel_id=1, source_target_pairs={{0,1},{1,2},{2,3},{3,4},{4,5},{5,6},{6,7},{7,8},{8,9},{9,10},{10,1... | collective-permute-start | bytes 3145736 | tf_op jit(solution)/shard_map/ppermute | solution.py:26
  96.2 1.9 %collective-permute-start.3 = (f32[2048,128]{1,0:T(8,128)S(1)}, f32[2048,128]{1,0:T(8,128)S(1)}, u32[]{:S(2)}, u32[]{:S(2)}) collective-permute-start(f32[2048,128]{1,0:T(8,128)S(1)} %get-tuple-element.8), channel_id=1, source_target_pairs={{1,0},{2,1},{3,2},{4,3},{5,4},{6,5},{7,6},{8,7},{9,8},{10,9},{11,1... | collective-permute-start | bytes 3145736 | tf_op jit(solution)/shard_map/ppermute | solution.py:26
  98.2 19.9 %collective-permute-done.2 = f32[2048,128]{1,0:T(8,128)S(1)} collective-permute-done((f32[2048,128]{1,0:T(8,128)S(1)}, f32[2048,128]{1,0:T(8,128)S(1)}, u32[]{:S(2)}, u32[]{:S(2)}) %collective-permute-start.2) | collective-permute-done | bytes 1048608 | tf_op jit(solution)/shard_map/ppermute | solution.py:26
  118.3 1.5 %pad_maximum_fusion = f32[2048,256]{1,0:T(8,128)} fusion(f32[2048,128]{1,0:T(8,128)S(1)} %get-tuple-element.18, f32[2048,128]{1,0:T(8,128)S(1)} %get-tuple-element.17), kind=kLoop, calls=%fused_computation.4 | loop fusion | flops 524288 | bytes 4194304 | tf_op jit(solution)/shard_map/concatenate | solution.py:96
  (52 shorter events, 11.6 us)
Async XLA Ops:
  7.2 16.3 %all-to-all-start = ((f32[8,128,128]{2,1,0:T(8,128)}), f32[8,128,128]{2,1,0:T(8,128)S(1)}, u32[]{:S(2)}, u32[]{:S(2)}) async-start(f32[8,128,128]{2,1,0:T(8,128)} %broadcast_in_dim.14), calls=%async_computation | async-start | bytes 1048576 | tf_op jit(solution)/shard_map/all_to_all | solution.py:15
  31.7 9.2 %copy-start.1 = (s32[128]{0:T(128)S(1)}, s32[128]{0:T(128)}, u32[]{:S(2)}) copy-start(s32[128]{0:T(128)} %param.3) | copy-start | bytes 1540
  33.6 31.4 %collective-permute-start = (f32[2048,128]{1,0:T(8,128)}, f32[2048,128]{1,0:T(8,128)S(1)}, u32[]{:S(2)}, u32[]{:S(2)}) collective-permute-start(f32[2048,128]{1,0:T(8,128)} %get-tuple-element.10), channel_id=1, source_target_pairs={{0,1},{1,2},{2,3},{3,4},{4,5},{5,6},{6,7},{7,8},{8,9},{9,10},{10,1... | collective-permute-start | bytes 3145736 | tf_op jit(solution)/shard_map/ppermute | solution.py:26
  38.9 26.1 %collective-permute-start.1 = (f32[2048,128]{1,0:T(8,128)S(1)}, f32[2048,128]{1,0:T(8,128)}, u32[]{:S(2)}, u32[]{:S(2)}) collective-permute-start(f32[2048,128]{1,0:T(8,128)S(1)} %get-tuple-element.11), channel_id=1, source_target_pairs={{1,0},{2,1},{3,2},{4,3},{5,4},{6,5},{7,6},{8,7},{9,8},{10,9},{11,1... | collective-permute-start | bytes 3145736 | tf_op jit(solution)/shard_map/ppermute | solution.py:26
  65.0 1.0 copy-start
  91.1 27.0 %collective-permute-start.2 = (f32[2048,128]{1,0:T(8,128)S(1)}, f32[2048,128]{1,0:T(8,128)S(1)}, u32[]{:S(2)}, u32[]{:S(2)}) collective-permute-start(f32[2048,128]{1,0:T(8,128)S(1)} %get-tuple-element.7), channel_id=1, source_target_pairs={{0,1},{1,2},{2,3},{3,4},{4,5},{5,6},{6,7},{7,8},{8,9},{9,10},{10,1... | collective-permute-start | bytes 3145736 | tf_op jit(solution)/shard_map/ppermute | solution.py:26
  96.2 21.8 %collective-permute-start.3 = (f32[2048,128]{1,0:T(8,128)S(1)}, f32[2048,128]{1,0:T(8,128)S(1)}, u32[]{:S(2)}, u32[]{:S(2)}) collective-permute-start(f32[2048,128]{1,0:T(8,128)S(1)} %get-tuple-element.8), channel_id=1, source_target_pairs={{1,0},{2,1},{3,2},{4,3},{5,4},{6,5},{7,6},{8,7},{9,8},{10,9},{11,1... | collective-permute-start | bytes 3145736 | tf_op jit(solution)/shard_map/ppermute | solution.py:26
where the time goes:
time: 120 us
  waiting for transfers between devices  48.2 us (40%)
  starting transfers between devices  21.7 us (18%)
  matrix products  19.9 us (17%)
  blocking collectives  12.4 us (10%)
  other arithmetic  10.5 us (9%)
  between operations  4.35 us (4%)
  local copies, waits for them, and re-layouts  2.65 us (2%)
    ppermute x4, waiting for transfers between devices, passed_along(): lax.ppermute(value, axis, [(source, source + steps) for source in range(i...  39.4 us
    ppermute x4, starting transfers between devices, passed_along(): lax.ppermute(value, axis, [(source, source + steps) for source in range(i...  14.2 us
    all_to_all x1, blocking collectives, copy_for_each(): return lax.all_to_all(copies, axis, split_axis=0, concat_axis=0, tiled=True)  12.4 us
    all_to_all x1, waiting for transfers between devices, copy_for_each(): return lax.all_to_all(copies, axis, split_axis=0, concat_axis=0, tiled=True)  8.83 us
    all_to_all x1, starting transfers between devices, copy_for_each(): return lax.all_to_all(copies, axis, split_axis=0, concat_axis=0, tiled=True)  7.47 us
    dot_general x2, matrix products, inner_rows(): lax.dot_general(first, second, (((0,), (0,)), ((), ())), precision=precise)  3.63 us
    select_n x2, other arithmetic, jacobi_step(): first = jnp.where(order_flag, upper, lower)  3.4 us
    dot_general x2, matrix products, jacobi_step(): jnp.dot(second - jnp.dot(first, coupling, precision=precise), right_inver...  2.94 us
  transfers between devices with their start and end apart: 5, of which 3 were waited for; matrix products, arithmetic and copies ran while one was open for 3% of the time, Pallas kernels for 0%

commit v1 on v0

v1 whole, which is shorter than its diff:
```python
import jax
import jax.numpy as jnp
from jax import lax
from jax.experimental import pallas as pl
from jax.experimental.pallas import tpu as pltpu
from jax.sharding import PartitionSpec as P

NS_ITERS = 3
BLK = 128
CHUNK = 512


def halves(x):
    hi = x.astype(jnp.bfloat16)
    lo = (x - hi.astype(jnp.float32)).astype(jnp.bfloat16)
    return hi, lo


def mm_parts(a, b, dims):
    def dot(p, q):
        return lax.dot_general(p, q, (dims, ((), ())), preferred_element_type=jnp.float32)

    return dot(a[0], b[0]) + (dot(a[0], b[1]) + dot(a[1], b[0]))


def mm(a, b, dims=((1,), (0,))):
    return mm_parts(halves(a), halves(b), dims)


def eye():
    i = lax.broadcasted_iota(jnp.int32, (BLK, BLK), 0)
    j = lax.broadcasted_iota(jnp.int32, (BLK, BLK), 1)
    return jnp.where(i == j, 1.0, 0.0).astype(jnp.float32)


def inverse_roots(mats):
    ident = eye()
    ys = [halves(m) for m in mats]
    fs = [1.5 * ident - 0.5 * m for m in mats]
    zs = fs
    for sweep in range(1, NS_ITERS):
        fps = [halves(f) for f in fs]
        ys = [halves(mm_parts(y, f, ((1,), (0,)))) for y, f in zip(ys, fps)]
        zps = [halves(z) for z in zs]
        fs = [1.5 * ident - 0.5 * mm_parts(z, y, ((1,), (0,))) for z, y in zip(zps, ys)]
        zs = [mm_parts(halves(f), z, ((1,), (0,))) for f, z in zip(fs, zps)]
    return [z * (5.0**-0.5) for z in zs]


def tangent(cross, sign):
    return cross * (sign * 2.0 / jnp.sqrt(jnp.sum(cross * cross) + 1e-06))


def gram(x, y):
    xs = jnp.concatenate(halves(x), axis=1)
    ys = jnp.concatenate(halves(y), axis=1)
    return lax.dot_general(xs, ys, (((0,), (0,)), ((), ())), preferred_element_type=jnp.float32)


def gram_kernel(get, copies_ref, acc_ref):
    step = pl.program_id(0)

    @pl.when(step == 0)
    def _():
        acc_ref[...] = jnp.zeros_like(acc_ref)

    acc_ref[...] += gram(*get())

    @pl.when(step == pl.num_programs(0) - 1)
    def _():
        acc = acc_ref[...]
        total = (acc[:BLK, :BLK] + acc[BLK:, BLK:]) + (acc[:BLK, BLK:] + acc[BLK:, :BLK])
        for k in range(copies_ref.shape[0]):
            copies_ref[k] = total


def cross_of_panel(panel, count):
    rows, cols = panel.shape

    def kernel(x_ref, copies_ref, acc_ref):
        gram_kernel(lambda: (x_ref[:, :BLK], x_ref[:, BLK:]), copies_ref, acc_ref)

    return pl.pallas_call(
        kernel,
        grid=(rows // CHUNK,),
        in_specs=[pl.BlockSpec((CHUNK, cols), lambda i: (i, 0))],
        out_specs=pl.BlockSpec((count, BLK, BLK), lambda i: (0, 0, 0)),
        out_shape=jax.ShapeDtypeStruct((count, BLK, BLK), jnp.float32),
        scratch_shapes=[pltpu.VMEM((2 * BLK, 2 * BLK), jnp.float32)],
        name="cross_of_panel",
    )(panel)


def cross_of_blocks(x, y, count):
    rows = x.shape[0]

    def kernel(x_ref, y_ref, copies_ref, acc_ref):
        gram_kernel(lambda: (x_ref[...], y_ref[...]), copies_ref, acc_ref)

    return pl.pallas_call(
        kernel,
        grid=(rows // CHUNK,),
        in_specs=[pl.BlockSpec((CHUNK, BLK), lambda i: (i, 0))] * 2,
        out_specs=pl.BlockSpec((count, BLK, BLK), lambda i: (0, 0, 0)),
        out_shape=jax.ShapeDtypeStruct((count, BLK, BLK), jnp.float32),
        scratch_shapes=[pltpu.VMEM((2 * BLK, 2 * BLK), jnp.float32)],
        name="cross_of_blocks",
    )(x, y)


def rotate_panel(scalars, slot_block, gathered, panel):
    rows, cols = panel.shape
    count = gathered.shape[0]

    def kernel(pos_ref, ids_ref, g_ref, x_ref, one_ref, two_ref, whi_ref, wlo_ref):
        @pl.when(pl.program_id(0) == 0)
        def _():
            pos = pos_ref[0]
            pairs = pos_ref[1]
            sign = jnp.where(ids_ref[pos] < ids_ref[pairs + pos], 1.0, -1.0)
            upper_first = (lax.rem(pos, 2) == 1) | (pos == 0)
            cross = g_ref[0]
            for k in range(1, count):
                cross = cross + g_ref[k]
            kappa = tangent(cross, sign)
            kp = halves(kappa)
            ident = eye()
            left = (ident + mm_parts(kp, kp, ((1,), (1,)))) / 5.0
            right = (ident + mm_parts(kp, kp, ((0,), (0,)))) / 5.0
            linv, rinv = inverse_roots([left, right])
            lk = mm(kappa, linv, ((0,), (0,)))
            kr = mm(kappa, rinv)
            up = jnp.concatenate([linv, lk], axis=0)
            low = jnp.concatenate([-kr, rinv], axis=0)
            w = jnp.concatenate(
                [jnp.where(upper_first, up, low), jnp.where(upper_first, low, up)], axis=1
            )
            hi, lo = halves(w)
            whi_ref[...] = hi
            wlo_ref[...] = lo

        out = mm_parts(halves(x_ref[...]), (whi_ref[...], wlo_ref[...]), ((1,), (0,)))
        one_ref[...] = out[:, :BLK]
        two_ref[...] = out[:, BLK:]

    return pl.pallas_call(
        kernel,
        grid_spec=pltpu.PrefetchScalarGridSpec(
            num_scalar_prefetch=2,
            grid=(rows // CHUNK,),
            in_specs=[
                pl.BlockSpec((count, BLK, BLK), lambda i, *_: (0, 0, 0)),
                pl.BlockSpec((CHUNK, cols), lambda i, *_: (i, 0)),
            ],
            out_specs=[pl.BlockSpec((CHUNK, BLK), lambda i, *_: (i, 0))] * 2,
            scratch_shapes=[pltpu.VMEM((2 * BLK, 2 * BLK), jnp.bfloat16)] * 2,
        ),
        out_shape=[jax.ShapeDtypeStruct((rows, BLK), jnp.float32)] * 2,
        name="rotate_panel",
    )(scalars, slot_block, gathered, panel)


def received_coefficients(cross, sign, swap):
    kappa = tangent(jnp.where(swap, cross.T, cross), jnp.where(swap, -sign, sign))
    kp = halves(kappa)
    right = (eye() + mm_parts(kp, kp, ((0,), (0,)))) / 5.0
    (rinv,) = inverse_roots([right])
    other = -mm(kappa, rinv)
    return jnp.where(swap, rinv, other), jnp.where(swap, other, rinv)


def rotate_received(scalars, slot_block, cross, local, received, primary, out):
    rows = local.shape[0]

    def kernel(pos_ref, ids_ref, m_ref, x_ref, y_ref, *rest):
        o_ref, whi_ref, wlo_ref = rest[-3:]

        @pl.when(pl.program_id(0) == 0)
        def _():
            pos = pos_ref[0]
            pairs = pos_ref[1]
            odd = lax.rem(pos, 2) == 1
            upper_first = odd | (pos == 0)
            if primary:
                mine = jnp.where(upper_first, pairs + pos, pos)
                theirs = jnp.where(
                    odd,
                    jnp.where(pos == 1, 0, pos - 2),
                    jnp.where(pos == pairs - 2, pairs - 1, pairs + pos + 2),
                )
                swap = pos == 1
                cross = m_ref[...]
            else:
                mine = jnp.where(upper_first, pos, pairs + pos)
                theirs = jnp.where(
                    odd,
                    jnp.where(pos == pairs - 1, pairs - 2, pairs + pos + 2),
                    jnp.where(pos == 0, pairs + 1, jnp.where(pos == 2, pairs, pos - 2)),
                )
                swap = pos == 0
                cross = m_ref[...].T
            sign = jnp.where(ids_ref[mine] < ids_ref[theirs], 1.0, -1.0)
            cx, cy = received_coefficients(cross, sign, swap)
            hi, lo = halves(jnp.concatenate([cx, cy], axis=0))
            whi_ref[...] = hi
            wlo_ref[...] = lo

        z = jnp.concatenate([x_ref[...], y_ref[...]], axis=1)
        o_ref[...] = mm_parts(halves(z), (whi_ref[...], wlo_ref[...]), ((1,), (0,)))

    block = pl.BlockSpec((CHUNK, BLK), lambda i, *_: (i, 0))
    half = 3 if primary else 2
    operands = [scalars, slot_block, cross, local, received]
    in_specs = [pl.BlockSpec((BLK, BLK), lambda i, *_: (0, 0)), block, block]
    aliases = {}
    if out is not None:
        operands.append(out)
        in_specs.append(pl.BlockSpec(memory_space=pl.ANY))
        aliases = {5: 0}
    return pl.pallas_call(
        kernel,
        grid_spec=pltpu.PrefetchScalarGridSpec(
            num_scalar_prefetch=2,
            grid=(rows // CHUNK,),
            in_specs=in_specs,
            out_specs=pl.BlockSpec((CHUNK, BLK), lambda i, s, *_: (i, s[half])),
            scratch_shapes=[pltpu.VMEM((2 * BLK, BLK), jnp.bfloat16)] * 2,
        ),
        out_shape=jax.ShapeDtypeStruct((rows, 2 * BLK), jnp.float32),
        input_output_aliases=aliases,
        name="rotate_primary" if primary else "rotate_secondary",
    )(*operands)


def exchange(copies):
    return lax.all_to_all(copies, "row", split_axis=0, concat_axis=0, tiled=True)


def per_device(panel, slot_block):
    count = lax.axis_size("row")
    pairs = lax.axis_size("pair")
    position = lax.axis_index("pair")
    odd = lax.rem(position, 2)
    scalars = jnp.stack([position, jnp.full_like(position, pairs), odd, 1 - odd]).astype(jnp.int32)
    there = [(q, q + 2) for q in range(1, pairs - 2, 2)] + [(q, q - 2) for q in range(2, pairs, 2)]
    there += [(0, 1), (pairs - 1, pairs - 2)]
    back = [(target, source) for source, target in there]

    one, two = rotate_panel(scalars, slot_block, exchange(cross_of_panel(panel, count)), panel)
    first = lax.ppermute(one, "pair", there)
    first, two = lax.optimization_barrier((first, two))
    second = lax.ppermute(two, "pair", back)
    cross = jnp.sum(exchange(cross_of_blocks(two, first, count)), axis=0)
    cross_back = lax.ppermute(cross, "pair", back)
    out = rotate_received(scalars, slot_block, cross, two, first, True, None)
    return rotate_received(scalars, slot_block, cross_back, one, second, False, out)


def solution(mesh):
    return jax.shard_map(
        per_device,
        mesh=mesh,
        in_specs=(P("row", "pair"), P()),
        out_specs=P("row", "pair"),
        check_vma=False,
    )
```

time: 120 us -> 111 us (0.925)
  the two profiles are of different devices: /device:TPU:1 before, /device:TPU:98 now
where the time goes in v1:
time: 111 us
  starting transfers between devices  32 us (29%)
  waiting for transfers between devices  31.8 us (29%)
  Pallas kernels  27.5 us (25%)
  blocking collectives  16.3 us (15%)
  local copies, waits for them, and re-layouts  2.44 us (2%)
    ppermute x1, waiting for transfers between devices, per_device(): first = lax.ppermute(one, 'pair', there)  21.3 us
    all_to_all x1, blocking collectives, exchange(): lax.all_to_all(copies, 'row', split_axis=0, concat_axis=0, tiled=True)  16.3 us
    ppermute x1, starting transfers between devices, per_device(): cross_back = lax.ppermute(cross, 'pair', back)  14.6 us
    pallas_call x2, Pallas kernels, rotate_received(): pl.pallas_call(kernel, grid_spec=pltpu.PrefetchScalarGridSpec(num_scalar_...  13 us
    all_to_all x1, waiting for transfers between devices, exchange(): lax.all_to_all(copies, 'row', split_axis=0, concat_axis=0, tiled=True)  10.4 us
    ppermute x1, starting transfers between devices, per_device(): second = lax.ppermute(two, 'pair', back)  8.05 us
    pallas_call x1, Pallas kernels, rotate_panel(): pl.pallas_call(kernel, grid_spec=pltpu.PrefetchScalarGridSpec(num_scalar_...  6.88 us
    all_to_all x1, starting transfers between devices, exchange(): lax.all_to_all(copies, 'row', split_axis=0, concat_axis=0, tiled=True)  6.03 us
  transfers between devices with their start and end apart: 4, of which 2 were waited for; matrix products, arithmetic and copies ran while one was open for 1% of the time, Pallas kernels for 9%

profile of v1, /device:TPU:98, one launch (start us, length us, event | category | flops | bytes accessed | tf_op | source)
XLA Modules:
  0.0 110.7 jit_solution(17788097050099552553)
XLA Ops:
  0.0 3.8 %cross_of_panel.1 = f32[8,128,128]{2,1,0:T(8,128)} custom-call(f32[2048,256]{1,0:T(8,128)} %x_ref.3), custom_call_target="tpu_custom_call" | custom-call | tf_op jit(solution)/shard_map/cross_of_panel/pallas_call | solution.py:83
  3.8 6.0 %all-to-all-start = ((f32[8,128,128]{2,1,0:T(8,128)}), f32[8,128,128]{2,1,0:T(8,128)S(1)}, u32[]{:S(2)}, u32[]{:S(2)}) async-start(f32[8,128,128]{2,1,0:T(8,128)} %cross_of_panel.1), calls=%async_computation | async-start | bytes 1048576 | tf_op jit(solution)/shard_map/all_to_all | solution.py:236
  9.9 0.6 pad_add_fusion.pos_ref
  10.5 10.4 %all-to-all-done.g_ref = f32[8,128,128]{2,1,0:T(8,128)S(1)} async-done(((f32[8,128,128]{2,1,0:T(8,128)}), f32[8,128,128]{2,1,0:T(8,128)S(1)}, u32[]{:S(2)}, u32[]{:S(2)}) %all-to-all-start) | async-done | bytes 524320 | tf_op jit(solution)/shard_map/all_to_all | solution.py:236
  20.9 0.0 copy-start.1
  20.9 0.8 copy-done.1
  21.7 6.9 %rotate_panel.1 = (f32[2048,128]{1,0:T(8,128)}, f32[2048,128]{1,0:T(8,128)}) custom-call(s32[4]{0:T(128)} %pad_add_fusion.pos_ref, s32[128]{0:T(128)} %ids_ref.5, f32[8,128,128]{2,1,0:T(8,128)} %copy-done.1, f32[2048,256]{1,0:T(8,128)} %x_ref.3), custom_call_target="tpu_custom_call" | custom-call | tf_op jit(solution)/shard_map/rotate_panel/pallas_call | solution.py:146
  28.6 3.3 %collective-permute-start = (f32[2048,128]{1,0:T(8,128)}, f32[2048,128]{1,0:T(8,128)S(1)}, u32[]{:S(2)}, u32[]{:S(2)}) collective-permute-start(f32[2048,128]{1,0:T(8,128)} %get-tuple-element.9.x_ref), channel_id=1, source_target_pairs={{1,3},{3,5},{5,7},{7,9},{9,11},{11,13},{13,15},{15,17},{17,19},{19... | collective-permute-start | bytes 3145736 | tf_op jit(solution)/shard_map/ppermute | solution.py:250
  31.9 21.3 %collective-permute-done.y_ref = f32[2048,128]{1,0:T(8,128)S(1)} collective-permute-done((f32[2048,128]{1,0:T(8,128)}, f32[2048,128]{1,0:T(8,128)S(1)}, u32[]{:S(2)}, u32[]{:S(2)}) %collective-permute-start) | collective-permute-done | bytes 1048608 | tf_op jit(solution)/shard_map/ppermute | solution.py:250
  53.2 8.0 %collective-permute-start.2 = (f32[2048,128]{1,0:T(8,128)}, f32[2048,128]{1,0:T(8,128)S(1)}, u32[]{:S(2)}, u32[]{:S(2)}) collective-permute-start(f32[2048,128]{1,0:T(8,128)} %get-tuple-element.11.x_ref), channel_id=1, source_target_pairs={{3,1},{5,3},{7,5},{9,7},{11,9},{13,11},{15,13},{17,15},{19,17},{21... | collective-permute-start | bytes 3145736 | tf_op jit(solution)/shard_map/ppermute | solution.py:252
  61.3 0.0 copy-done
  61.3 3.8 %cross_of_blocks.1 = f32[8,128,128]{2,1,0:T(8,128)} custom-call(f32[2048,128]{1,0:T(8,128)} %get-tuple-element.11.x_ref, f32[2048,128]{1,0:T(8,128)} %copy-done), custom_call_target="tpu_custom_call" | custom-call | tf_op jit(solution)/shard_map/cross_of_blocks/pallas_call | solution.py:100
  65.1 16.3 %all_to_all.10 = f32[8,128,128]{2,1,0:T(8,128)S(1)} all-to-all(f32[8,128,128]{2,1,0:T(8,128)} %cross_of_blocks.1), channel_id=1, replica_groups=mesh['row'=8,'pair'=64] {'row'}, dimensions={0} | all-to-all | bytes 1048576 | tf_op jit(solution)/shard_map/all_to_all | solution.py:236
  81.4 0.0 copy-start.3
  81.4 14.6 %collective-permute-start.1 = (f32[128,128]{1,0:T(8,128)S(1)}, f32[128,128]{1,0:T(8,128)S(1)}, u32[]{:S(2)}, u32[]{:S(2)}) collective-permute-start(f32[128,128]{1,0:T(8,128)S(1)} %reduce_sum.9.m_ref), channel_id=1, source_target_pairs={{3,1},{5,3},{7,5},{9,7},{11,9},{13,11},{15,13},{17,15},{19,17},{21... | collective-permute-start | bytes 196616 | tf_op jit(solution)/shard_map/ppermute | solution.py:254
  96.0 0.0 copy-done.3
  96.0 6.5 %rotate_primary.1.rest_0_ = f32[2048,256]{1,0:T(8,128)} custom-call(s32[4]{0:T(128)} %pad_add_fusion.pos_ref, s32[128]{0:T(128)} %ids_ref.5, f32[128,128]{1,0:T(8,128)} %copy-done.3, f32[2048,128]{1,0:T(8,128)} %get-tuple-element.11.x_ref, f32[2048,128]{1,0:T(8,128)} %copy-done), custom_call_target="tpu_custom_call" | custom-call | tf_op jit(solution)/shard_map/rotate_primary/pallas_call | solution.py:220
  102.6 0.0 collective-permute-done.1.m_ref
  102.6 0.0 copy-start.4
  102.6 0.0 collective-permute-done.2.y_ref
  102.6 0.6 copy-done.4
  103.2 0.0 copy-start.2
  103.2 1.0 copy-done.2
  104.2 6.5 %rotate_secondary.1 = f32[2048,256]{1,0:T(8,128)} custom-call(s32[4]{0:T(128)} %pad_add_fusion.pos_ref, s32[128]{0:T(128)} %ids_ref.5, f32[128,128]{1,0:T(8,128)} %copy-done.4, f32[2048,128]{1,0:T(8,128)} %get-tuple-element.9.x_ref, f32[2048,128]{1,0:T(8,128)} %copy-done.2, f32[2048,256]{1,0:T(8,128)} %rotate_primary.1.rest_0_), custom_call_target="tpu_custom_call", output_to_operand_aliasing={{}: (5, {})} | custom-call | tf_op jit(solution)/shard_map/rotate_secondary/pallas_call | solution.py:220
  (2 shorter events, 0.0 us)
Async XLA Ops:
  3.8 17.1 %all-to-all-start = ((f32[8,128,128]{2,1,0:T(8,128)}), f32[8,128,128]{2,1,0:T(8,128)S(1)}, u32[]{:S(2)}, u32[]{:S(2)}) async-start(f32[8,128,128]{2,1,0:T(8,128)} %cross_of_panel.1), calls=%async_computation | async-start | bytes 1048576 | tf_op jit(solution)/shard_map/all_to_all | solution.py:236
  20.9 0.8 copy-start.1
  28.6 24.6 %collective-permute-start = (f32[2048,128]{1,0:T(8,128)}, f32[2048,128]{1,0:T(8,128)S(1)}, u32[]{:S(2)}, u32[]{:S(2)}) collective-permute-start(f32[2048,128]{1,0:T(8,128)} %get-tuple-element.9.x_ref), channel_id=1, source_target_pairs={{1,3},{3,5},{5,7},{7,9},{9,11},{11,13},{13,15},{15,17},{17,19},{19... | collective-permute-start | bytes 3145736 | tf_op jit(solution)/shard_map/ppermute | solution.py:250
  53.2 8.1 %copy-start = (f32[2048,128]{1,0:T(8,128)}, f32[2048,128]{1,0:T(8,128)S(1)}, u32[]{:S(2)}) copy-start(f32[2048,128]{1,0:T(8,128)S(1)} %collective-permute-done.y_ref) | copy-start | bytes 3145732
  53.2 49.3 %collective-permute-start.2 = (f32[2048,128]{1,0:T(8,128)}, f32[2048,128]{1,0:T(8,128)S(1)}, u32[]{:S(2)}, u32[]{:S(2)}) collective-permute-start(f32[2048,128]{1,0:T(8,128)} %get-tuple-element.11.x_ref), channel_id=1, source_target_pairs={{3,1},{5,3},{7,5},{9,7},{11,9},{13,11},{15,13},{17,15},{19,17},{21... | collective-permute-start | bytes 3145736 | tf_op jit(solution)/shard_map/ppermute | solution.py:252
  81.4 14.6 %copy-start.3 = (f32[128,128]{1,0:T(8,128)}, f32[128,128]{1,0:T(8,128)S(1)}, u32[]{:S(2)}) copy-start(f32[128,128]{1,0:T(8,128)S(1)} %reduce_sum.9.m_ref) | copy-start | bytes 196612
  81.4 21.1 %collective-permute-start.1 = (f32[128,128]{1,0:T(8,128)S(1)}, f32[128,128]{1,0:T(8,128)S(1)}, u32[]{:S(2)}, u32[]{:S(2)}) collective-permute-start(f32[128,128]{1,0:T(8,128)S(1)} %reduce_sum.9.m_ref), channel_id=1, source_target_pairs={{3,1},{5,3},{7,5},{9,7},{11,9},{13,11},{15,13},{17,15},{19,17},{21... | collective-permute-start | bytes 196616 | tf_op jit(solution)/shard_map/ppermute | solution.py:254
  102.6 0.6 copy-start.4
  103.2 1.0 copy-start.2

commit v2 on v0

v2 whole, which is shorter than its diff:
```python
import functools

import jax
import jax.numpy as jnp
from jax import lax
from jax.experimental import pallas as pl
from jax.experimental.pallas import tpu as pltpu
from jax.sharding import PartitionSpec as P

NS_ITERS = 3
BLK = 128
CHUNK = 256
TAIL = 256
VMEM = pl.BlockSpec(memory_space=pltpu.VMEM)
SMEM = pl.BlockSpec(memory_space=pltpu.SMEM)
ANY = pl.BlockSpec(memory_space=pl.ANY)
NN = ((1,), (0,))
TN = ((0,), (0,))
NT = ((1,), (1,))


def call(kernel, out_shape, in_specs, out_specs, flops, scratch=(), aliases=None):
    return pl.pallas_call(
        kernel,
        out_shape=out_shape,
        in_specs=in_specs,
        out_specs=out_specs,
        scratch_shapes=list(scratch),
        input_output_aliases=aliases or {},
        compiler_params=pltpu.CompilerParams(vmem_limit_bytes=16 << 20),
        cost_estimate=pl.CostEstimate(flops=flops, bytes_accessed=2 << 20, transcendentals=0),
    )


def halves(x):
    hi = x.astype(jnp.bfloat16)
    lo = (x - hi.astype(jnp.float32)).astype(jnp.bfloat16)
    return hi, lo


def mm_parts(a, b, dims=NN):
    def dot(p, q):
        return lax.dot_general(p, q, (dims, ((), ())), preferred_element_type=jnp.float32)

    return dot(a[0], b[0]) + (dot(a[0], b[1]) + dot(a[1], b[0]))


def mm(a, b, dims=NN):
    return mm_parts(halves(a), halves(b), dims)


def eye():
    i = lax.broadcasted_iota(jnp.int32, (BLK, BLK), 0)
    j = lax.broadcasted_iota(jnp.int32, (BLK, BLK), 1)
    return jnp.where(i == j, 1.0, 0.0).astype(jnp.float32)


def inverse_roots(mats):
    ident = eye()
    ys = [halves(m) for m in mats]
    fs = [1.5 * ident - 0.5 * m for m in mats]
    zs = fs
    for _ in range(1, NS_ITERS):
        fps = [halves(f) for f in fs]
        ys = [halves(mm_parts(y, f)) for y, f in zip(ys, fps)]
        zps = [halves(z) for z in zs]
        fs = [1.5 * ident - 0.5 * mm_parts(z, y) for z, y in zip(zps, ys)]
        zs = [mm_parts(halves(f), z) for f, z in zip(fs, zps)]
    return [z * (5.0**-0.5) for z in zs]


def tangent(cross, sign):
    return cross * (sign * 2.0 / jnp.sqrt(jnp.sum(cross * cross) + 1e-06))


def gram(pairs):
    acc = None
    for x, y in pairs:
        xs = jnp.concatenate(halves(x), axis=1)
        ys = jnp.concatenate(halves(y), axis=1)
        part = lax.dot_general(xs, ys, (TN, ((), ())), preferred_element_type=jnp.float32)
        acc = part if acc is None else acc + part
    return acc


def fold(acc):
    return (acc[:BLK, :BLK] + acc[BLK:, BLK:]) + (acc[:BLK, BLK:] + acc[BLK:, :BLK])


def chunks(rows):
    return [pl.ds(r, min(CHUNK, rows - r)) for r in range(0, rows, CHUNK)]


def cross_of_panel(panel, count):
    rows = panel.shape[0]

    def kernel(x_ref, copies_ref):
        total = fold(gram((x_ref[c, :BLK], x_ref[c, BLK:]) for c in chunks(rows)))
        for k in range(count):
            copies_ref[k] = total

    shape = jax.ShapeDtypeStruct((count, BLK, BLK), jnp.float32)
    return call(kernel, shape, [VMEM], VMEM, rows * BLK * BLK * 8)(panel)


def cross_head(local, received):
    rows = received.shape[0]

    def kernel(x_ref, y_ref, acc_ref):
        acc_ref[...] = gram((x_ref[c, :], y_ref[c, :]) for c in chunks(rows))

    shape = jax.ShapeDtypeStruct((2 * BLK, 2 * BLK), jnp.float32)
    return call(kernel, shape, [VMEM] * 2, VMEM, rows * BLK * BLK * 8)(local, received)


def cross_tail(acc, local, received, count):
    rows = received.shape[0]
    base = local.shape[0] - rows

    def kernel(acc_ref, x_ref, y_ref, copies_ref):
        x_tail = x_ref.at[base:, :]
        total = fold(acc_ref[...] + gram((x_tail[c, :], y_ref[c, :]) for c in chunks(rows)))
        for k in range(count):
            copies_ref[k] = total

    shape = jax.ShapeDtypeStruct((count, BLK, BLK), jnp.float32)
    return call(kernel, shape, [VMEM] * 3, VMEM, rows * BLK * BLK * 8)(acc, local, received)


def total_of(parts):
    def kernel(p_ref, o_ref):
        total = p_ref[0]
        for k in range(1, parts.shape[0]):
            total = total + p_ref[k]
        o_ref[...] = total

    shape = jax.ShapeDtypeStruct(parts.shape[1:], parts.dtype)
    return call(kernel, shape, [VMEM], VMEM, parts.size)(parts)


def rotate_panel(slot_block, gathered, panel, pairs):
    rows = panel.shape[0]
    count = gathered.shape[0]
    head = rows - TAIL

    def kernel(ids_ref, g_ref, x_ref, head_ref, tail_ref, two_ref):
        pos = lax.axis_index("pair")
        sign = jnp.where(ids_ref[pos] < ids_ref[pairs + pos], 1.0, -1.0)
        upper_first = (lax.rem(pos, 2) == 1) | (pos == 0)
        cross = g_ref[0]
        for k in range(1, count):
            cross = cross + g_ref[k]
        kappa = tangent(cross, sign)
        kp = halves(kappa)
        ident = eye()
        left = (ident + mm_parts(kp, kp, NT)) / 5.0
        right = (ident + mm_parts(kp, kp, TN)) / 5.0
        linv, rinv = inverse_roots([left, right])
        up = jnp.concatenate([linv, mm(kappa, linv, TN)], axis=0)
        low = jnp.concatenate([-mm(kappa, rinv), rinv], axis=0)
        w = jnp.concatenate(
            [jnp.where(upper_first, up, low), jnp.where(upper_first, low, up)], axis=1
        )
        wp = halves(w)
        for c in chunks(rows):
            out = mm_parts(halves(x_ref[c, :]), wp)
            if c.start < head:
                head_ref[c, :] = out[:, :BLK]
            else:
                tail_ref[pl.ds(c.start - head, c.size), :] = out[:, :BLK]
            two_ref[c, :] = out[:, BLK:]

    shapes = [jax.ShapeDtypeStruct((n, BLK), jnp.float32) for n in (head, TAIL, rows)]
    return call(
        kernel, shapes, [SMEM, VMEM, VMEM], [VMEM] * 3, rows * BLK * BLK * 24
    )(slot_block, gathered, panel)


def rotate_received(slot_block, crosses, locals_, received, out, pairs, primary):
    rows = sum(x.shape[0] for x in received)
    n_loc, n_rec = len(locals_), len(received)

    def rows_of(refs, c):
        start = c.start
        for ref in refs:
            if start < ref.shape[0]:
                return ref[pl.ds(start, c.size), :]
            start -= ref.shape[0]

    def kernel(*refs):
        ids_ref, m_ref, n_ref = refs[:3]
        x_refs = refs[3 : 3 + n_loc]
        y_refs = refs[3 + n_loc : 3 + n_loc + n_rec]
        o_ref, buf_ref, sems = refs[-3:]
        pos = lax.axis_index("pair")
        odd = lax.rem(pos, 2) == 1
        upper_first = odd | (pos == 0)
        if primary:
            mine = jnp.where(upper_first, pairs + pos, pos)
            theirs = jnp.where(
                odd,
                jnp.where(pos == 1, 0, pos - 2),
                jnp.where(pos == pairs - 2, pairs - 1, pairs + pos + 2),
            )
            swap = pos == 1
            column = jnp.where(odd, 0, BLK)
            cross = m_ref[...] + n_ref[...]
        else:
            mine = jnp.where(upper_first, pos, pairs + pos)
            theirs = jnp.where(
                odd,
                jnp.where(pos == pairs - 1, pairs - 2, pairs + pos + 2),
                jnp.where(pos == 0, pairs + 1, jnp.where(pos == 2, pairs, pos - 2)),
            )
            swap = pos == 0
            column = jnp.where(odd, BLK, 0)
            cross = (m_ref[...] + n_ref[...]).T
        sign = jnp.where(ids_ref[mine] < ids_ref[theirs], 1.0, -1.0)
        kappa = tangent(jnp.where(swap, cross.T, cross), jnp.where(swap, -sign, sign))
        kp = halves(kappa)
        (rinv,) = inverse_roots([(eye() + mm_parts(kp, kp, TN)) / 5.0])
        other = -mm(kappa, rinv)
        w = jnp.concatenate(
            [jnp.where(swap, rinv, other), jnp.where(swap, other, rinv)], axis=0
        )
        wp = halves(w)
        column = pl.multiple_of(column, BLK)
        copies = []
        for i, c in enumerate(chunks(rows)):
            z = jnp.concatenate([rows_of(x_refs, c), rows_of(y_refs, c)], axis=1)
            buf_ref[c, :] = mm_parts(halves(z), wp)
            copy = pltpu.make_async_copy(
                buf_ref.at[c, :], o_ref.at[c, pl.ds(column, BLK)], sems.at[i]
            )
            copy.start()
            copies.append(copy)
        for copy in copies:
            copy.wait()

    operands = [slot_block, *crosses, *locals_, *received]
    in_specs = [SMEM] + [VMEM] * (len(operands) - 1)
    aliases = {}
    if out is not None:
        aliases = {len(operands): 0}
        operands.append(out)
        in_specs.append(ANY)
    return call(
        kernel,
        jax.ShapeDtypeStruct((rows, 2 * BLK), jnp.float32),
        in_specs,
        ANY,
        rows * BLK * BLK * 12,
        scratch=[
            pltpu.VMEM((rows, BLK), jnp.float32),
            pltpu.SemaphoreType.DMA((rows // CHUNK,)),
        ],
        aliases=aliases,
    )(*operands)


def per_device(panel, slot_block):
    count = lax.axis_size("row")
    pairs = lax.axis_size("pair")
    half = count // 2
    there = [(q, q + 2) for q in range(1, pairs - 2, 2)] + [(q, q - 2) for q in range(2, pairs, 2)]
    there += [(0, 1), (pairs - 1, pairs - 2)]
    back = [(target, source) for source, target in there]
    across = [(r, (r + half) % count) for r in range(count)]
    back_across = [
        (r * pairs + source, s * pairs + target) for r, s in across for source, target in back
    ]
    near = [list(range(half)), list(range(half, count))]
    exchange = functools.partial(
        lax.all_to_all, axis_name="row", split_axis=0, concat_axis=0, tiled=True
    )

    gathered = exchange(cross_of_panel(panel, count))
    one_head, one_tail, two = rotate_panel(slot_block, gathered, panel, pairs)
    got_head = lax.ppermute(one_head, "pair", there)
    got_tail = lax.ppermute(one_tail, "pair", there)
    got_head, two = lax.optimization_barrier((got_head, two))
    second = lax.ppermute(two, "pair", back)
    acc = cross_head(two, got_head)
    part = total_of(
        exchange(cross_tail(acc, two, got_tail, half), axis_index_groups=near)
    )
    other = lax.ppermute(part, "row", across)
    back_near = lax.ppermute(part, "pair", back)
    back_far = lax.ppermute(part, ("row", "pair"), back_across)
    out = rotate_received(slot_block, [part, other], [two], [got_head, got_tail], None, pairs, True)
    return rotate_received(
        slot_block,
        [back_near, back_far],
        [one_head, one_tail],
        [second],
        out,
        pairs,
        False,
    )


def solution(mesh):
    return jax.shard_map(
        per_device,
        mesh=mesh,
        in_specs=(P("row", "pair"), P()),
        out_specs=P("row", "pair"),
        check_vma=False,
    )
```

time: 120 us -> 99.8 us (0.83)
  the two profiles are of different devices: /device:TPU:1 before, /device:TPU:448 now
where the time goes in v2:
time: 99.8 us; the launch traced here: 99.5 us
  waiting for transfers between devices  34.8 us (35%)
  blocking collectives  27.6 us (28%)
  starting transfers between devices  23.4 us (23%)
  Pallas kernels  12 us (12%)
  local copies, waits for them, and re-layouts  1.59 us (2%)
    ppermute x1, waiting for transfers between devices, per_device(): got_head = lax.ppermute(one_head, 'pair', there)  20.1 us
    all_to_all x1, blocking collectives, per_device(): gathered = exchange(cross_of_panel(panel, count))  18.3 us
    ppermute x1, waiting for transfers between devices, per_device(): got_tail = lax.ppermute(one_tail, 'pair', there)  14.7 us
    all_to_all x1, blocking collectives, per_device(): exchange(cross_tail(acc, two, got_tail, half), axis_index_groups=near)  9.31 us
    ppermute x1, starting transfers between devices, per_device(): back_near = lax.ppermute(part, 'pair', back)  7.66 us
    pallas_call x2, Pallas kernels, rotate_received(): call(kernel, jax.ShapeDtypeStruct((rows, 2 * BLK), jnp.float32), in_specs...  7.61 us
    ppermute x1, starting transfers between devices, per_device(): got_tail = lax.ppermute(one_tail, 'pair', there)  4.82 us
    pallas_call x1, Pallas kernels, rotate_panel(): call(kernel, shapes, [SMEM, VMEM, VMEM], [VMEM] * 3, rows * BLK * BLK * 24)  3.19 us
  transfers between devices with their start and end apart: 6, of which 2 were waited for; matrix products, arithmetic and copies ran while one was open for 0% of the time, Pallas kernels for 5%

profile of v2, /device:TPU:448, one launch (start us, length us, event | category | flops | bytes accessed | tf_op | source)
XLA Modules:
  0.0 99.5 jit_solution(7449364403200207016)
XLA Ops:
  0.0 0.0 copy-start
  0.0 1.6 %copy-done = f32[2048,256]{1,0:T(8,128)S(1)} copy-done((f32[2048,256]{1,0:T(8,128)S(1)}, f32[2048,256]{1,0:T(8,128)}, u32[]{:S(2)}) %copy-start) | copy-done | bytes 2097176
  1.6 0.0 copy-start.1
  1.6 0.5 shard_map.28
  2.1 18.3 %all_to_all.10.g_ref = f32[8,128,128]{2,1,0:T(8,128)S(1)} all-to-all(f32[8,128,128]{2,1,0:T(8,128)S(1)} %shard_map.28), channel_id=1, replica_groups=mesh['row'=8,'pair'=64] {'row'}, dimensions={0} | all-to-all | bytes 1048576 | tf_op jit(solution)/shard_map/all_to_all | solution.py:277
  20.3 0.0 copy-done.1
  20.3 3.2 %shard_map.29 = (f32[1792,128]{1,0:T(8,128)S(1)}, f32[256,128]{1,0:T(8,128)S(1)}, f32[2048,128]{1,0:T(8,128)S(1)}) custom-call(s32[128]{0:T(128)S(1)} %copy-done.1, f32[8,128,128]{2,1,0:T(8,128)S(1)} %all_to_all.10.g_ref, f32[2048,256]{1,0:T(8,128)S(1)} %copy-done), custom_call_target="tpu_custom_call" | custom-call | flops 805306368 | bytes 2097152 | tf_op jit(solution)/shard_map/pallas_call | solution.py:174
  23.5 2.9 %collective-permute-start = (f32[1792,128]{1,0:T(8,128)S(1)}, f32[1792,128]{1,0:T(8,128)S(1)}, u32[]{:S(2)}, u32[]{:S(2)}) collective-permute-start(f32[1792,128]{1,0:T(8,128)S(1)} %get-tuple-element.10.refs_3_), channel_id=1, source_target_pairs={{1,3},{3,5},{5,7},{7,9},{9,11},{11,13},{13,15},{15,17},{17,19},{19... | collective-permute-start | bytes 2752520 | tf_op jit(solution)/shard_map/ppermute | solution.py:279
  26.5 20.1 %collective-permute-done.y_ref.refs_4_ = f32[1792,128]{1,0:T(8,128)S(1)} collective-permute-done((f32[1792,128]{1,0:T(8,128)S(1)}, f32[1792,128]{1,0:T(8,128)S(1)}, u32[]{:S(2)}, u32[]{:S(2)}) %collective-permute-start) | collective-permute-done | bytes 917536 | tf_op jit(solution)/shard_map/ppermute | solution.py:279
  46.6 1.9 %collective-permute-start.4 = (f32[2048,128]{1,0:T(8,128)S(1)}, f32[2048,128]{1,0:T(8,128)S(1)}, u32[]{:S(2)}, u32[]{:S(2)}) collective-permute-start(f32[2048,128]{1,0:T(8,128)S(1)} %get-tuple-element.12.x_ref.refs_3_), channel_id=1, source_target_pairs={{3,1},{5,3},{7,5},{9,7},{11,9},{13,11},{15,13},{17,15},{19,17},{21... | collective-permute-start | bytes 3145736 | tf_op jit(solution)/shard_map/ppermute | solution.py:282
  48.6 4.8 %collective-permute-start.1 = (f32[256,128]{1,0:T(8,128)S(1)}, f32[256,128]{1,0:T(8,128)S(1)}, u32[]{:S(2)}, u32[]{:S(2)}) collective-permute-start(f32[256,128]{1,0:T(8,128)S(1)} %get-tuple-element.14.refs_4_), channel_id=1, source_target_pairs={{1,3},{3,5},{5,7},{7,9},{9,11},{11,13},{13,15},{15,17},{17,19},{19... | collective-permute-start | bytes 393224 | tf_op jit(solution)/shard_map/ppermute | solution.py:280
  53.4 0.5 shard_map.30.acc_ref
  53.9 14.7 %collective-permute-done.1.y_ref.refs_5_ = f32[256,128]{1,0:T(8,128)S(1)} collective-permute-done((f32[256,128]{1,0:T(8,128)S(1)}, f32[256,128]{1,0:T(8,128)S(1)}, u32[]{:S(2)}, u32[]{:S(2)}) %collective-permute-start.1) | collective-permute-done | bytes 131104 | tf_op jit(solution)/shard_map/ppermute | solution.py:280
  68.5 0.2 shard_map.31
  68.8 9.3 %all_to_all.11.p_ref = f32[4,128,128]{2,1,0:T(8,128)S(1)} all-to-all(f32[4,128,128]{2,1,0:T(8,128)S(1)} %shard_map.31), channel_id=1, replica_groups={{0,64,128,192},{256,320,384,448},{1,65,129,193},{257,321,385,449},{2,66..., dimensions={0} | all-to-all | bytes 524288 | tf_op jit(solution)/shard_map/all_to_all | solution.py:285
  78.1 3.1 %collective-permute-start.5 = (f32[128,128]{1,0:T(8,128)S(1)}, f32[128,128]{1,0:T(8,128)S(1)}, u32[]{:S(2)}, u32[]{:S(2)}) collective-permute-start(f32[128,128]{1,0:T(8,128)S(1)} %shard_map.32.refs_1_), channel_id=1, source_target_pairs={{0,256},{64,320},{128,384},{192,448},{256,0},{320,64},{384,128},{4... | collective-permute-start | bytes 196616 | tf_op jit(solution)/shard_map/ppermute | solution.py:287
  81.2 2.9 %collective-permute-start.3 = (f32[128,128]{1,0:T(8,128)S(1)}, f32[128,128]{1,0:T(8,128)S(1)}, u32[]{:S(2)}, u32[]{:S(2)}) collective-permute-start(f32[128,128]{1,0:T(8,128)S(1)} %shard_map.32.refs_1_), channel_id=1, source_target_pairs={{3,257},{5,259},{7,261},{9,263},{11,265},{13,267},{15,269},{17,271... | collective-permute-start | bytes 196616 | tf_op jit(solution)/shard_map/ppermute | solution.py:289
  84.1 7.7 %collective-permute-start.2 = (f32[128,128]{1,0:T(8,128)S(1)}, f32[128,128]{1,0:T(8,128)S(1)}, u32[]{:S(2)}, u32[]{:S(2)}) collective-permute-start(f32[128,128]{1,0:T(8,128)S(1)} %shard_map.32.refs_1_), channel_id=1, source_target_pairs={{3,1},{5,3},{7,5},{9,7},{11,9},{13,11},{15,13},{17,15},{19,17},{21... | collective-permute-start | bytes 196616 | tf_op jit(solution)/shard_map/ppermute | solution.py:288
  91.8 0.0 collective-permute-done.5.refs_2_
  91.8 3.8 %shard_map.33.refs_6_ = f32[2048,256]{1,0:T(8,128)} custom-call(s32[128]{0:T(128)S(1)} %copy-done.1, f32[128,128]{1,0:T(8,128)S(1)} %shard_map.32.refs_1_, f32[128,128]{1,0:T(8,128)S(1)} %collective-permute-done.5.refs_2_, f32[2048,128]{1,0:T(8,128)S(1)} %get-tuple-element.12.x_ref.refs_3_, f32[1792,128]{1,0:T(8,128)S(1)} %collective-permute-done.y_ref.refs_4_, ...), custom_call_target="tpu_custom_call" | custom-call | flops 402653184 | bytes 2097152 | tf_op jit(solution)/shard_map/pallas_call | solution.py:247
  95.6 0.0 collective-permute-done.3.refs_2_
  95.6 0.0 collective-permute-done.2.refs_1_
  95.7 0.0 collective-permute-done.4.refs_5_
  95.7 3.8 %shard_map.34 = f32[2048,256]{1,0:T(8,128)} custom-call(s32[128]{0:T(128)S(1)} %copy-done.1, f32[128,128]{1,0:T(8,128)S(1)} %collective-permute-done.2.refs_1_, f32[128,128]{1,0:T(8,128)S(1)} %collective-permute-done.3.refs_2_, f32[1792,128]{1,0:T(8,128)S(1)} %get-tuple-element.10.refs_3_, ...), custom_call_target="tpu_custom_call", output_to_operand_aliasing={{}: (6, {})} | custom-call | flops 402653184 | bytes 2097152 | tf_op jit(solution)/shard_map/pallas_call | solution.py:247
  (1 shorter events, 0.0 us)
Async XLA Ops:
  0.0 1.6 %copy-start = (f32[2048,256]{1,0:T(8,128)S(1)}, f32[2048,256]{1,0:T(8,128)}, u32[]{:S(2)}) copy-start(f32[2048,256]{1,0:T(8,128)} %x_ref.3) | copy-start | bytes 6291460
  1.6 18.8 %copy-start.1 = (s32[128]{0:T(128)S(1)}, s32[128]{0:T(128)}, u32[]{:S(2)}) copy-start(s32[128]{0:T(128)} %refs_0_.3) | copy-start | bytes 1540
  23.5 23.1 %collective-permute-start = (f32[1792,128]{1,0:T(8,128)S(1)}, f32[1792,128]{1,0:T(8,128)S(1)}, u32[]{:S(2)}, u32[]{:S(2)}) collective-permute-start(f32[1792,128]{1,0:T(8,128)S(1)} %get-tuple-element.10.refs_3_), channel_id=1, source_target_pairs={{1,3},{3,5},{5,7},{7,9},{9,11},{11,13},{13,15},{15,17},{17,19},{19... | collective-permute-start | bytes 2752520 | tf_op jit(solution)/shard_map/ppermute | solution.py:279
  46.6 49.0 %collective-permute-start.4 = (f32[2048,128]{1,0:T(8,128)S(1)}, f32[2048,128]{1,0:T(8,128)S(1)}, u32[]{:S(2)}, u32[]{:S(2)}) collective-permute-start(f32[2048,128]{1,0:T(8,128)S(1)} %get-tuple-element.12.x_ref.refs_3_), channel_id=1, source_target_pairs={{3,1},{5,3},{7,5},{9,7},{11,9},{13,11},{15,13},{17,15},{19,17},{21... | collective-permute-start | bytes 3145736 | tf_op jit(solution)/shard_map/ppermute | solution.py:282
  48.6 20.0 %collective-permute-start.1 = (f32[256,128]{1,0:T(8,128)S(1)}, f32[256,128]{1,0:T(8,128)S(1)}, u32[]{:S(2)}, u32[]{:S(2)}) collective-permute-start(f32[256,128]{1,0:T(8,128)S(1)} %get-tuple-element.14.refs_4_), channel_id=1, source_target_pairs={{1,3},{3,5},{5,7},{7,9},{9,11},{11,13},{13,15},{15,17},{17,19},{19... | collective-permute-start | bytes 393224 | tf_op jit(solution)/shard_map/ppermute | solution.py:280
  78.1 13.7 %collective-permute-start.5 = (f32[128,128]{1,0:T(8,128)S(1)}, f32[128,128]{1,0:T(8,128)S(1)}, u32[]{:S(2)}, u32[]{:S(2)}) collective-permute-start(f32[128,128]{1,0:T(8,128)S(1)} %shard_map.32.refs_1_), channel_id=1, source_target_pairs={{0,256},{64,320},{128,384},{192,448},{256,0},{320,64},{384,128},{4... | collective-permute-start | bytes 196616 | tf_op jit(solution)/shard_map/ppermute | solution.py:287
  81.2 14.4 %collective-permute-start.3 = (f32[128,128]{1,0:T(8,128)S(1)}, f32[128,128]{1,0:T(8,128)S(1)}, u32[]{:S(2)}, u32[]{:S(2)}) collective-permute-start(f32[128,128]{1,0:T(8,128)S(1)} %shard_map.32.refs_1_), channel_id=1, source_target_pairs={{3,257},{5,259},{7,261},{9,263},{11,265},{13,267},{15,269},{17,271... | collective-permute-start | bytes 196616 | tf_op jit(solution)/shard_map/ppermute | solution.py:289
  84.1 11.5 %collective-permute-start.2 = (f32[128,128]{1,0:T(8,128)S(1)}, f32[128,128]{1,0:T(8,128)S(1)}, u32[]{:S(2)}, u32[]{:S(2)}) collective-permute-start(f32[128,128]{1,0:T(8,128)S(1)} %shard_map.32.refs_1_), channel_id=1, source_target_pairs={{3,1},{5,3},{7,5},{9,7},{11,9},{13,11},{15,13},{17,15},{19,17},{21... | collective-permute-start | bytes 196616 | tf_op jit(solution)/shard_map/ppermute | solution.py:288

commit v3 on v2

v3 whole, which is shorter than its diff:
```python
import functools

import jax
import jax.numpy as jnp
from jax import lax
from jax.experimental import pallas as pl
from jax.experimental.pallas import tpu as pltpu
from jax.sharding import PartitionSpec as P

NS_ITERS = 3
BLK = 128
CHUNK = 256
SPIN = 1500
VMEM = pl.BlockSpec(memory_space=pltpu.VMEM)
SMEM = pl.BlockSpec(memory_space=pltpu.SMEM)
ANY = pl.BlockSpec(memory_space=pl.ANY)
NN = ((1,), (0,))
TN = ((0,), (0,))
NT = ((1,), (1,))


def call(kernel, out_shape, in_specs, out_specs, flops, scratch=(), aliases=None):
    return pl.pallas_call(
        kernel,
        out_shape=out_shape,
        in_specs=in_specs,
        out_specs=out_specs,
        scratch_shapes=list(scratch),
        input_output_aliases=aliases or {},
        compiler_params=pltpu.CompilerParams(vmem_limit_bytes=16 << 20),
        cost_estimate=pl.CostEstimate(flops=flops, bytes_accessed=2 << 20, transcendentals=0),
    )


def halves(x):
    hi = x.astype(jnp.bfloat16)
    lo = (x - hi.astype(jnp.float32)).astype(jnp.bfloat16)
    return hi, lo


def mm_parts(a, b, dims=NN):
    def dot(p, q):
        return lax.dot_general(p, q, (dims, ((), ())), preferred_element_type=jnp.float32)

    return dot(a[0], b[0]) + (dot(a[0], b[1]) + dot(a[1], b[0]))


def dot(a, b, dims=NN):
    return lax.dot_general(a, b, (dims, ((), ())), preferred_element_type=jnp.float32)


def mm_narrow(a, b):
    ah, al = halves(a)
    wide = dot(ah, jnp.concatenate(b, axis=1))
    return (wide[:, :BLK] + wide[:, BLK:]) + dot(al, b[0])


def mm(a, b, dims=NN):
    return mm_parts(halves(a), halves(b), dims)


def eye():
    i = lax.broadcasted_iota(jnp.int32, (BLK, BLK), 0)
    j = lax.broadcasted_iota(jnp.int32, (BLK, BLK), 1)
    return jnp.where(i == j, 1.0, 0.0).astype(jnp.float32)


def inverse_roots(mats):
    ident = eye()
    ys = [halves(m) for m in mats]
    fs = [1.5 * ident - 0.5 * m for m in mats]
    zs = fs
    for _ in range(1, NS_ITERS):
        fps = [halves(f) for f in fs]
        ys = [halves(mm_parts(y, f)) for y, f in zip(ys, fps)]
        zps = [halves(z) for z in zs]
        fs = [1.5 * ident - 0.5 * mm_parts(z, y) for z, y in zip(zps, ys)]
        zs = [mm_parts(halves(f), z) for f, z in zip(fs, zps)]
    return [z * (5.0**-0.5) for z in zs]


def tangent(cross, sign):
    return cross * (sign * 2.0 / jnp.sqrt(jnp.sum(cross * cross) + 1e-06))


def gram(pairs):
    acc = None
    for x, y in pairs:
        xs = jnp.concatenate(halves(x), axis=1)
        ys = jnp.concatenate(halves(y), axis=1)
        part = lax.dot_general(xs, ys, (TN, ((), ())), preferred_element_type=jnp.float32)
        acc = part if acc is None else acc + part
    return acc


def fold(acc):
    return (acc[:BLK, :BLK] + acc[BLK:, BLK:]) + (acc[:BLK, BLK:] + acc[BLK:, :BLK])


def chunks(rows):
    return [pl.ds(r, min(CHUNK, rows - r)) for r in range(0, rows, CHUNK)]


def cross_of_panel(panel, count):
    rows = panel.shape[0]

    def kernel(x_ref, copies_ref):
        total = fold(gram((x_ref[c, :BLK], x_ref[c, BLK:]) for c in chunks(rows)))
        for k in range(count):
            copies_ref[k] = total

    shape = jax.ShapeDtypeStruct((count, BLK, BLK), jnp.float32)
    return call(kernel, shape, [VMEM], VMEM, rows * BLK * BLK * 8)(panel)


def cross_of_blocks(local, received, count):
    rows = received.shape[0]

    def kernel(x_ref, y_ref, copies_ref):
        total = fold(gram((x_ref[c, :], y_ref[c, :]) for c in chunks(rows)))
        for k in range(count):
            copies_ref[k] = total

    shape = jax.ShapeDtypeStruct((count, BLK, BLK), jnp.float32)
    return call(kernel, shape, [VMEM] * 2, VMEM, rows * BLK * BLK * 8)(local, received)


def hold_ends(got, block, pairs):
    def kernel(g_ref, x_ref, o_ref, s_ref):
        pos = lax.axis_index("pair")
        at_end = (pos == 0) | (pos == pairs - 1)

        @pl.when(at_end)
        def _():
            s_ref[...] = lax.fori_loop(0, SPIN, lambda i, x: x * 0.5 + 1.0, g_ref[0:8, :])

    shapes = [
        jax.ShapeDtypeStruct(block.shape, block.dtype),
        jax.ShapeDtypeStruct((8, BLK), block.dtype),
    ]
    return call(kernel, shapes, [VMEM, ANY], [ANY, VMEM], 1000, aliases={1: 0})(got, block)[0]


def total_of(parts, copies):
    def kernel(*refs):
        total = None
        for ref in refs[:-1]:
            for k in range(ref.shape[0]):
                total = ref[k] if total is None else total + ref[k]
        for k in range(copies):
            refs[-1][k] = total

    shape = jax.ShapeDtypeStruct((copies, BLK, BLK), jnp.float32)
    return call(kernel, shape, [VMEM] * len(parts), VMEM, BLK * BLK * 4)(*parts)


def rotate_panel(slot_block, gathered, panel, pairs):
    rows = panel.shape[0]
    count = gathered.shape[0]

    def kernel(ids_ref, g_ref, x_ref, one_ref, two_ref):
        pos = lax.axis_index("pair")
        sign = jnp.where(ids_ref[pos] < ids_ref[pairs + pos], 1.0, -1.0)
        upper_first = (lax.rem(pos, 2) == 1) | (pos == 0)
        cross = g_ref[0]
        for k in range(1, count):
            cross = cross + g_ref[k]
        kappa = tangent(cross, sign)
        kp = halves(kappa)
        ident = eye()
        left = (ident + mm_parts(kp, kp, NT)) / 5.0
        right = (ident + mm_parts(kp, kp, TN)) / 5.0
        linv, rinv = inverse_roots([left, right])
        up = jnp.concatenate([linv, mm(kappa, linv, TN)], axis=0)
        low = jnp.concatenate([-mm(kappa, rinv), rinv], axis=0)
        w = jnp.concatenate(
            [jnp.where(upper_first, up, low), jnp.where(upper_first, low, up)], axis=1
        )
        wp = halves(w)
        for c in chunks(rows):
            out = mm_parts(halves(x_ref[c, :]), wp)
            one_ref[c, :] = out[:, :BLK]
            two_ref[c, :] = out[:, BLK:]

    shapes = [jax.ShapeDtypeStruct((n, BLK), jnp.float32) for n in (rows, rows)]
    return call(
        kernel, shapes, [SMEM, VMEM, VMEM], [VMEM] * 2, rows * BLK * BLK * 24
    )(slot_block, gathered, panel)


def rotate_pairs(slot_block, crosses, locals_, received, pairs):
    rows = locals_[0].shape[0]
    steps = rows // CHUNK

    def kernel(ids_ref, a_ref, b_ref, c_ref, d_ref, x1_ref, y1_ref, x2_ref, y2_ref, *rest):
        o_ref, buf_ref, sems = rest
        pos = lax.axis_index("pair")
        odd = lax.rem(pos, 2) == 1
        upper_first = odd | (pos == 0)
        mine = [jnp.where(upper_first, pairs + pos, pos), jnp.where(upper_first, pos, pairs + pos)]
        theirs = [
            jnp.where(
                odd,
                jnp.where(pos == 1, 0, pos - 2),
                jnp.where(pos == pairs - 2, pairs - 1, pairs + pos + 2),
            ),
            jnp.where(
                odd,
                jnp.where(pos == pairs - 1, pairs - 2, pairs + pos + 2),
                jnp.where(pos == 0, pairs + 1, jnp.where(pos == 2, pairs, pos - 2)),
            ),
        ]
        swaps = [pos == 1, pos == 0]
        crosses = [a_ref[0] + b_ref[0], c_ref[0] + d_ref[0]]
        kappas = []
        for k in range(2):
            flip = swaps[k] if k == 0 else jnp.logical_not(swaps[k])
            sign = jnp.where(ids_ref[mine[k]] < ids_ref[theirs[k]], 1.0, -1.0)
            cross = jnp.where(flip, crosses[k].T, crosses[k])
            kappas.append(tangent(cross, jnp.where(swaps[k], -sign, sign)))
        ident = eye()
        rights = []
        for kappa in kappas:
            kp = halves(kappa)
            rights.append((ident + mm_parts(kp, kp, TN)) / 5.0)
        rinvs = inverse_roots(rights)
        wps = []
        for k in range(2):
            other = -mm(kappas[k], rinvs[k])
            w = [jnp.where(swaps[k], rinvs[k], other), jnp.where(swaps[k], other, rinvs[k])]
            wps.append(halves(jnp.concatenate(w, axis=0)))
        columns = [jnp.where(odd, 0, BLK), jnp.where(odd, BLK, 0)]
        copies = []
        for i, c in enumerate(chunks(rows)):
            for k, (x_ref, y_ref) in enumerate(((x1_ref, y1_ref), (x2_ref, y2_ref))):
                z = jnp.concatenate([x_ref[c, :], y_ref[c, :]], axis=1)
                buf_ref[k, c, :] = mm_narrow(z, wps[k])
                column = pl.multiple_of(columns[k], BLK)
                copy = pltpu.make_async_copy(
                    buf_ref.at[k, c, :], o_ref.at[c, pl.ds(column, BLK)], sems.at[k, i]
                )
                copy.start()
                copies.append(copy)
        for copy in copies:
            copy.wait()

    operands = [slot_block, *crosses, locals_[0], received[0], locals_[1], received[1]]
    return call(
        kernel,
        jax.ShapeDtypeStruct((rows, 2 * BLK), jnp.float32),
        [SMEM] + [VMEM] * 8,
        ANY,
        rows * BLK * BLK * 24,
        scratch=[
            pltpu.VMEM((2, rows, BLK), jnp.float32),
            pltpu.SemaphoreType.DMA((2, steps)),
        ],
    )(*operands)


def per_device(panel, slot_block):
    count = lax.axis_size("row")
    pairs = lax.axis_size("pair")
    half = count // 2
    there = [(q, q + 2) for q in range(1, pairs - 2, 2)] + [(q, q - 2) for q in range(2, pairs, 2)]
    there += [(0, 1), (pairs - 1, pairs - 2)]
    back = [(target, source) for source, target in there]
    across = [(r, (r + half) % count) for r in range(count)]
    back_across = [
        (r * pairs + source, s * pairs + target) for r, s in across for source, target in back
    ]
    near = [list(range(half)), list(range(half, count))]
    exchange = functools.partial(
        lax.all_to_all, axis_name="row", split_axis=0, concat_axis=0, tiled=True
    )

    gathered = exchange(cross_of_panel(panel, count))
    one, two = rotate_panel(slot_block, gathered, panel, pairs)
    first = lax.ppermute(one, "pair", there)
    two = hold_ends(first, two, pairs)
    second = lax.ppermute(two, "pair", back)
    partial = cross_of_blocks(two, first, half)
    part = total_of([exchange(partial, axis_index_groups=near)], 1)
    back_near = lax.ppermute(part, "pair", back)
    back_far = lax.ppermute(part, ("row", "pair"), back_across)
    other = lax.ppermute(part, "row", across)
    return rotate_pairs(
        slot_block, [part, other, back_near, back_far], [two, one], [first, second], pairs
    )


def solution(mesh):
    return jax.shard_map(
        per_device,
        mesh=mesh,
        in_specs=(P("row", "pair"), P()),
        out_specs=P("row", "pair"),
        check_vma=False,
    )
```

time: 99.8 us -> 85.3 us (0.85)
  the two profiles are of different devices: /device:TPU:448 before, /device:TPU:66 now
where the time goes in v3:
time: 85.3 us; the launch traced here: 85 us
  blocking collectives  26.7 us (31%)
  waiting for transfers between devices  25.5 us (30%)
  starting transfers between devices  22.1 us (26%)
  Pallas kernels  9.08 us (11%)
  local copies, waits for them, and re-layouts  1.59 us (2%)
    ppermute x1, waiting for transfers between devices, per_device(): first = lax.ppermute(one, 'pair', there)  21.5 us
    all_to_all x1, blocking collectives, per_device(): gathered = exchange(cross_of_panel(panel, count))  17.4 us
    all_to_all x1, blocking collectives, per_device(): part = total_of([exchange(partial, axis_index_groups=near)], 1)  9.31 us
    ppermute x1, starting transfers between devices, per_device(): back_near = lax.ppermute(part, 'pair', back)  7.41 us
    ppermute x1, starting transfers between devices, per_device(): second = lax.ppermute(two, 'pair', back)  5.73 us
    pallas_call x1, Pallas kernels, rotate_pairs(): call(kernel, jax.ShapeDtypeStruct((rows, 2 * BLK), jnp.float32), [SMEM] +...  4.3 us
    ppermute x1, starting transfers between devices, per_device(): other = lax.ppermute(part, 'row', across)  3.66 us
    ppermute x1, starting transfers between devices, per_device(): first = lax.ppermute(one, 'pair', there)  3.34 us
  transfers between devices with their start and end apart: 5, of which 3 were waited for; matrix products, arithmetic and copies ran while one was open for 0% of the time, Pallas kernels for 1%

profile of v3, /device:TPU:66, one launch (start us, length us, event | category | flops | bytes accessed | tf_op | source)
XLA Modules:
  0.0 85.0 jit_solution(9970864566207875176)
XLA Ops:
  0.0 0.0 copy-start
  0.0 1.6 %copy-done = f32[2048,256]{1,0:T(8,128)S(1)} copy-done((f32[2048,256]{1,0:T(8,128)S(1)}, f32[2048,256]{1,0:T(8,128)}, u32[]{:S(2)}) %copy-start) | copy-done | bytes 2097176
  1.6 0.0 copy-start.1
  1.6 0.5 shard_map.28
  2.1 17.4 %all_to_all.10.g_ref = f32[8,128,128]{2,1,0:T(8,128)S(1)} all-to-all(f32[8,128,128]{2,1,0:T(8,128)S(1)} %shard_map.28), channel_id=1, replica_groups=mesh['row'=8,'pair'=64] {'row'}, dimensions={0} | all-to-all | bytes 1048576 | tf_op jit(solution)/shard_map/all_to_all | solution.py:277
  19.4 0.0 copy-done.1
  19.4 3.2 %shard_map.29 = (f32[2048,128]{1,0:T(8,128)S(1)}, f32[2048,128]{1,0:T(8,128)S(1)}) custom-call(s32[128]{0:T(128)S(1)} %copy-done.1, f32[8,128,128]{2,1,0:T(8,128)S(1)} %all_to_all.10.g_ref, f32[2048,256]{1,0:T(8,128)S(1)} %copy-done), custom_call_target="tpu_custom_call" | custom-call | flops 805306368 | bytes 2097152 | tf_op jit(solution)/shard_map/pallas_call | solution.py:186
  22.6 3.3 %collective-permute-start = (f32[2048,128]{1,0:T(8,128)S(1)}, f32[2048,128]{1,0:T(8,128)S(1)}, u32[]{:S(2)}, u32[]{:S(2)}) collective-permute-start(f32[2048,128]{1,0:T(8,128)S(1)} %get-tuple-element.8.x2_ref), channel_id=1, source_target_pairs={{1,3},{3,5},{5,7},{7,9},{9,11},{11,13},{13,15},{15,17},{17,19},{19... | collective-permute-start | bytes 3145736 | tf_op jit(solution)/shard_map/ppermute | solution.py:279
  26.0 21.5 %collective-permute-done.g_ref.y_ref.y1_ref = f32[2048,128]{1,0:T(8,128)S(1)} collective-permute-done((f32[2048,128]{1,0:T(8,128)S(1)}, f32[2048,128]{1,0:T(8,128)S(1)}, u32[]{:S(2)}, u32[]{:S(2)}) %collective-permute-start) | collective-permute-done | bytes 1048608 | tf_op jit(solution)/shard_map/ppermute | solution.py:279
  47.5 0.6 shard_map.30
  48.1 5.7 %collective-permute-start.4 = (f32[2048,128]{1,0:T(8,128)S(1)}, f32[2048,128]{1,0:T(8,128)S(1)}, u32[]{:S(2)}, u32[]{:S(2)}) collective-permute-start(f32[2048,128]{1,0:T(8,128)S(1)} %get-tuple-element.10.x_ref.x1_ref), channel_id=1, source_target_pairs={{3,1},{5,3},{7,5},{9,7},{11,9},{13,11},{15,13},{17,15},{19,17},{21... | collective-permute-start | bytes 3145736 | tf_op jit(solution)/shard_map/ppermute | solution.py:281
  53.8 0.5 shard_map.31
  54.3 9.3 %all_to_all.11.refs_0_ = f32[4,128,128]{2,1,0:T(8,128)S(1)} all-to-all(f32[4,128,128]{2,1,0:T(8,128)S(1)} %shard_map.31), channel_id=1, replica_groups={{0,64,128,192},{256,320,384,448},{1,65,129,193},{257,321,385,449},{2,66..., dimensions={0} | all-to-all | bytes 524288 | tf_op jit(solution)/shard_map/all_to_all | solution.py:283
  63.7 1.9 %collective-permute-start.3 = (f32[1,128,128]{2,1,0:T(8,128)S(1)}, f32[1,128,128]{2,1,0:T(8,128)S(1)}, u32[]{:S(2)}, u32[]{:S(2)}) collective-permute-start(f32[1,128,128]{2,1,0:T(8,128)S(1)} %shard_map.32.a_ref), channel_id=1, source_target_pairs={{3,257},{5,259},{7,261},{9,263},{11,265},{13,267},{15,269},{17,271... | collective-permute-start | bytes 196616 | tf_op jit(solution)/shard_map/ppermute | solution.py:285
  65.6 7.4 %collective-permute-start.2 = (f32[1,128,128]{2,1,0:T(8,128)S(1)}, f32[1,128,128]{2,1,0:T(8,128)S(1)}, u32[]{:S(2)}, u32[]{:S(2)}) collective-permute-start(f32[1,128,128]{2,1,0:T(8,128)S(1)} %shard_map.32.a_ref), channel_id=1, source_target_pairs={{3,1},{5,3},{7,5},{9,7},{11,9},{13,11},{15,13},{17,15},{19,17},{21... | collective-permute-start | bytes 196616 | tf_op jit(solution)/shard_map/ppermute | solution.py:284
  73.0 3.7 %collective-permute-start.1 = (f32[1,128,128]{2,1,0:T(8,128)S(1)}, f32[1,128,128]{2,1,0:T(8,128)S(1)}, u32[]{:S(2)}, u32[]{:S(2)}) collective-permute-start(f32[1,128,128]{2,1,0:T(8,128)S(1)} %shard_map.32.a_ref), channel_id=1, source_target_pairs={{0,256},{64,320},{128,384},{192,448},{256,0},{320,64},{384,128},{4... | collective-permute-start | bytes 196616 | tf_op jit(solution)/shard_map/ppermute | solution.py:286
  76.7 0.0 collective-permute-done.3.d_ref
  76.7 1.3 %collective-permute-done.2.c_ref = f32[1,128,128]{2,1,0:T(8,128)S(1)} collective-permute-done((f32[1,128,128]{2,1,0:T(8,128)S(1)}, f32[1,128,128]{2,1,0:T(8,128)S(1)}, u32[]{:S(2)}, u32[]{:S(2)}) %collective-permute-start.2) | collective-permute-done | bytes 65568 | tf_op jit(solution)/shard_map/ppermute | solution.py:284
  78.0 2.7 %collective-permute-done.1.b_ref = f32[1,128,128]{2,1,0:T(8,128)S(1)} collective-permute-done((f32[1,128,128]{2,1,0:T(8,128)S(1)}, f32[1,128,128]{2,1,0:T(8,128)S(1)}, u32[]{:S(2)}, u32[]{:S(2)}) %collective-permute-start.1) | collective-permute-done | bytes 65568 | tf_op jit(solution)/shard_map/ppermute | solution.py:286
  80.7 0.0 collective-permute-done.4.y2_ref
  80.7 4.3 %shard_map.33 = f32[2048,256]{1,0:T(8,128)} custom-call(s32[128]{0:T(128)S(1)} %copy-done.1, f32[1,128,128]{2,1,0:T(8,128)S(1)} %shard_map.32.a_ref, f32[1,128,128]{2,1,0:T(8,128)S(1)} %collective-permute-done.1.b_ref, f32[1,128,128]{2,1,0:T(8,128)S(1)} %collective-permute-done.2.c_ref, f32[1,128,128]{2,1,0:T(8,128)S(1)} %collective-permute-done.3.d_ref, ...), custom_call_target="tpu_custom_call" | custom-call | flops 805306368 | bytes 2097152 | tf_op jit(solution)/shard_map/pallas_call | solution.py:248
  (1 shorter events, 0.0 us)
Async XLA Ops:
  0.0 1.6 %copy-start = (f32[2048,256]{1,0:T(8,128)S(1)}, f32[2048,256]{1,0:T(8,128)}, u32[]{:S(2)}) copy-start(f32[2048,256]{1,0:T(8,128)} %x_ref.3) | copy-start | bytes 6291460
  1.6 17.9 %copy-start.1 = (s32[128]{0:T(128)S(1)}, s32[128]{0:T(128)}, u32[]{:S(2)}) copy-start(s32[128]{0:T(128)} %ids_ref.3) | copy-start | bytes 1540
  22.6 24.9 %collective-permute-start = (f32[2048,128]{1,0:T(8,128)S(1)}, f32[2048,128]{1,0:T(8,128)S(1)}, u32[]{:S(2)}, u32[]{:S(2)}) collective-permute-start(f32[2048,128]{1,0:T(8,128)S(1)} %get-tuple-element.8.x2_ref), channel_id=1, source_target_pairs={{1,3},{3,5},{5,7},{7,9},{9,11},{11,13},{13,15},{15,17},{17,19},{19... | collective-permute-start | bytes 3145736 | tf_op jit(solution)/shard_map/ppermute | solution.py:279
  48.1 32.6 %collective-permute-start.4 = (f32[2048,128]{1,0:T(8,128)S(1)}, f32[2048,128]{1,0:T(8,128)S(1)}, u32[]{:S(2)}, u32[]{:S(2)}) collective-permute-start(f32[2048,128]{1,0:T(8,128)S(1)} %get-tuple-element.10.x_ref.x1_ref), channel_id=1, source_target_pairs={{3,1},{5,3},{7,5},{9,7},{11,9},{13,11},{15,13},{17,15},{19,17},{21... | collective-permute-start | bytes 3145736 | tf_op jit(solution)/shard_map/ppermute | solution.py:281
  63.7 13.0 %collective-permute-start.3 = (f32[1,128,128]{2,1,0:T(8,128)S(1)}, f32[1,128,128]{2,1,0:T(8,128)S(1)}, u32[]{:S(2)}, u32[]{:S(2)}) collective-permute-start(f32[1,128,128]{2,1,0:T(8,128)S(1)} %shard_map.32.a_ref), channel_id=1, source_target_pairs={{3,257},{5,259},{7,261},{9,263},{11,265},{13,267},{15,269},{17,271... | collective-permute-start | bytes 196616 | tf_op jit(solution)/shard_map/ppermute | solution.py:285
  65.6 12.4 %collective-permute-start.2 = (f32[1,128,128]{2,1,0:T(8,128)S(1)}, f32[1,128,128]{2,1,0:T(8,128)S(1)}, u32[]{:S(2)}, u32[]{:S(2)}) collective-permute-start(f32[1,128,128]{2,1,0:T(8,128)S(1)} %shard_map.32.a_ref), channel_id=1, source_target_pairs={{3,1},{5,3},{7,5},{9,7},{11,9},{13,11},{15,13},{17,15},{19,17},{21... | collective-permute-start | bytes 196616 | tf_op jit(solution)/shard_map/ppermute | solution.py:284
  73.0 7.7 %collective-permute-start.1 = (f32[1,128,128]{2,1,0:T(8,128)S(1)}, f32[1,128,128]{2,1,0:T(8,128)S(1)}, u32[]{:S(2)}, u32[]{:S(2)}) collective-permute-start(f32[1,128,128]{2,1,0:T(8,128)S(1)} %shard_map.32.a_ref), channel_id=1, source_target_pairs={{0,256},{64,320},{128,384},{192,448},{256,0},{320,64},{384,128},{4... | collective-permute-start | bytes 196616 | tf_op jit(solution)/shard_map/ppermute | solution.py:286

commit v4 on v3

--- a/solution.py
+++ b/solution.py
@@ -113,32 +113,28 @@
     return call(kernel, shape, [VMEM], VMEM, rows * BLK * BLK * 8)(panel)
 
 
-def cross_of_blocks(local, received, count):
+def cross_of_blocks(local, received, count, pairs):
     rows = received.shape[0]
 
-    def kernel(x_ref, y_ref, copies_ref):
+    def kernel(x_ref, y_ref, copies_ref, o_ref):
         total = fold(gram((x_ref[c, :], y_ref[c, :]) for c in chunks(rows)))
         for k in range(count):
             copies_ref[k] = total
-
-    shape = jax.ShapeDtypeStruct((count, BLK, BLK), jnp.float32)
-    return call(kernel, shape, [VMEM] * 2, VMEM, rows * BLK * BLK * 8)(local, received)
-
-
-def hold_ends(got, block, pairs):
-    def kernel(g_ref, x_ref, o_ref, s_ref):
         pos = lax.axis_index("pair")
-        at_end = (pos == 0) | (pos == pairs - 1)
-
-        @pl.when(at_end)
+
+        @pl.when((pos == 1) | (pos == pairs - 2))
         def _():
-            s_ref[...] = lax.fori_loop(0, SPIN, lambda i, x: x * 0.5 + 1.0, g_ref[0:8, :])
+            start = jnp.full((8, BLK), pos, jnp.float32)
+            turned = lax.fori_loop(0, SPIN, lambda i, x: x * 0.5 + 1.0, start)
+            copies_ref[0, 0:8, :] = jnp.where(turned > 1000.0, turned, total[0:8, :])
 
     shapes = [
-        jax.ShapeDtypeStruct(block.shape, block.dtype),
-        jax.ShapeDtypeStruct((8, BLK), block.dtype),
+        jax.ShapeDtypeStruct((count, BLK, BLK), jnp.float32),
+        jax.ShapeDtypeStruct(local.shape, local.dtype),
     ]
-    return call(kernel, shapes, [VMEM, ANY], [ANY, VMEM], 1000, aliases={1: 0})(got, block)[0]
+    return call(
+        kernel, shapes, [VMEM] * 2, [VMEM, ANY], rows * BLK * BLK * 8, aliases={0: 1}
+    )(local, received)
 
 
 def total_of(parts, copies):
@@ -154,11 +150,11 @@
     return call(kernel, shape, [VMEM] * len(parts), VMEM, BLK * BLK * 4)(*parts)
 
 
-def rotate_panel(slot_block, gathered, panel, pairs):
+def rotate_first(slot_block, gathered, panel, pairs):
     rows = panel.shape[0]
     count = gathered.shape[0]
 
-    def kernel(ids_ref, g_ref, x_ref, one_ref, two_ref):
+    def kernel(ids_ref, g_ref, x_ref, two_ref, w_ref):
         pos = lax.axis_index("pair")
         sign = jnp.where(ids_ref[pos] < ids_ref[pairs + pos], 1.0, -1.0)
         upper_first = (lax.rem(pos, 2) == 1) | (pos == 0)
@@ -173,19 +169,30 @@
         linv, rinv = inverse_roots([left, right])
         up = jnp.concatenate([linv, mm(kappa, linv, TN)], axis=0)
         low = jnp.concatenate([-mm(kappa, rinv), rinv], axis=0)
-        w = jnp.concatenate(
-            [jnp.where(upper_first, up, low), jnp.where(upper_first, low, up)], axis=1
-        )
-        wp = halves(w)
+        w_ref[...] = jnp.where(upper_first, up, low)
+        wp = halves(jnp.where(upper_first, low, up))
         for c in chunks(rows):
-            out = mm_parts(halves(x_ref[c, :]), wp)
-            one_ref[c, :] = out[:, :BLK]
-            two_ref[c, :] = out[:, BLK:]
-
-    shapes = [jax.ShapeDtypeStruct((n, BLK), jnp.float32) for n in (rows, rows)]
+            two_ref[c, :] = mm_narrow(x_ref[c, :], wp)
+
+    shapes = [
+        jax.ShapeDtypeStruct((rows, BLK), jnp.float32),
+        jax.ShapeDtypeStruct((2 * BLK, BLK), jnp.float32),
+    ]
     return call(
-        kernel, shapes, [SMEM, VMEM, VMEM], [VMEM] * 2, rows * BLK * BLK * 24
+        kernel, shapes, [SMEM, VMEM, VMEM], [VMEM] * 2, rows * BLK * BLK * 12
     )(slot_block, gathered, panel)
+
+
+def rotate_other(panel, factors):
+    rows = panel.shape[0]
+
+    def kernel(x_ref, w_ref, one_ref):
+        wp = halves(w_ref[...])
+        for c in chunks(rows):
+            one_ref[c, :] = mm_narrow(x_ref[c, :], wp)
+
+    shape = jax.ShapeDtypeStruct((rows, BLK), jnp.float32)
+    return call(kernel, shape, [VMEM] * 2, VMEM, rows * BLK * BLK * 12)(panel, factors)
 
 
 def rotate_pairs(slot_block, crosses, locals_, received, pairs):
@@ -214,7 +221,7 @@
         crosses = [a_ref[0] + b_ref[0], c_ref[0] + d_ref[0]]
         kappas = []
         for k in range(2):
-            flip = swaps[k] if k == 0 else jnp.logical_not(swaps[k])
+            flip = swaps[k] if k == 1 else jnp.logical_not(swaps[k])
             sign = jnp.where(ids_ref[mine[k]] < ids_ref[theirs[k]], 1.0, -1.0)
             cross = jnp.where(flip, crosses[k].T, crosses[k])
             kappas.append(tangent(cross, jnp.where(swaps[k], -sign, sign)))
@@ -267,7 +274,7 @@
     back = [(target, source) for source, target in there]
     across = [(r, (r + half) % count) for r in range(count)]
     back_across = [
-        (r * pairs + source, s * pairs + target) for r, s in across for source, target in back
+        (r * pairs + source, s * pairs + target) for r, s in across for source, target in there
     ]
     near = [list(range(half)), list(range(half, count))]
     exchange = functools.partial(
@@ -275,17 +282,17 @@
     )
 
     gathered = exchange(cross_of_panel(panel, count))
-    one, two = rotate_panel(slot_block, gathered, panel, pairs)
-    first = lax.ppermute(one, "pair", there)
-    two = hold_ends(first, two, pairs)
-    second = lax.ppermute(two, "pair", back)
-    partial = cross_of_blocks(two, first, half)
+    two, factors = rotate_first(slot_block, gathered, panel, pairs)
+    first = lax.ppermute(two, "pair", back)
+    one = rotate_other(panel, factors)
+    partial, one = cross_of_blocks(one, first, half, pairs)
+    second = lax.ppermute(one, "pair", there)
     part = total_of([exchange(partial, axis_index_groups=near)], 1)
-    back_near = lax.ppermute(part, "pair", back)
+    back_near = lax.ppermute(part, "pair", there)
     back_far = lax.ppermute(part, ("row", "pair"), back_across)
     other = lax.ppermute(part, "row", across)
     return rotate_pairs(
-        slot_block, [part, other, back_near, back_far], [two, one], [first, second], pairs
+        slot_block, [back_near, back_far, part, other], [two, one], [second, first], pairs
     )
 
 

time: 85.3 us -> 83.8 us (0.982)
  the two profiles are of different devices: /device:TPU:66 before, /device:TPU:96 now
where the time goes in v4:
time: 83.8 us; the launch traced here: 83.5 us
  waiting for transfers between devices  30.4 us (36%)
  blocking collectives  27.6 us (33%)
  starting transfers between devices  15 us (18%)
  Pallas kernels  8.83 us (11%)
  local copies, waits for them, and re-layouts  1.59 us (2%)
    ppermute x1, waiting for transfers between devices, per_device(): first = lax.ppermute(two, 'pair', back)  22.2 us
    all_to_all x1, blocking collectives, per_device(): gathered = exchange(cross_of_panel(panel, count))  18.3 us
    all_to_all x1, blocking collectives, per_device(): part = total_of([exchange(partial, axis_index_groups=near)], 1)  9.3 us
    ppermute x1, waiting for transfers between devices, per_device(): back_near = lax.ppermute(part, 'pair', there)  6.28 us
    ppermute x1, starting transfers between devices, per_device(): back_far = lax.ppermute(part, ('row', 'pair'), back_across)  4.32 us
    pallas_call x1, Pallas kernels, rotate_pairs(): call(kernel, jax.ShapeDtypeStruct((rows, 2 * BLK), jnp.float32), [SMEM] +...  4.3 us
    ppermute x1, starting transfers between devices, per_device(): other = lax.ppermute(part, 'row', across)  3.53 us
    pallas_call x1, Pallas kernels, rotate_first(): call(kernel, shapes, [SMEM, VMEM, VMEM], [VMEM] * 2, rows * BLK * BLK * 12)  2.84 us
  transfers between devices with their start and end apart: 5, of which 4 were waited for; matrix products, arithmetic and copies ran while one was open for 0% of the time, Pallas kernels for 1%

profile of v4, /device:TPU:96, one launch (start us, length us, event | category | flops | bytes accessed | tf_op | source)
XLA Modules:
  0.0 83.5 jit_solution(2724780975487513256)
XLA Ops:
  0.0 0.0 copy-start
  0.0 1.6 %copy-done = f32[2048,256]{1,0:T(8,128)S(1)} copy-done((f32[2048,256]{1,0:T(8,128)S(1)}, f32[2048,256]{1,0:T(8,128)}, u32[]{:S(2)}) %copy-start) | copy-done | bytes 2097176
  1.6 0.0 copy-start.1
  1.6 0.5 shard_map.28
  2.1 18.3 %all_to_all.10.g_ref = f32[8,128,128]{2,1,0:T(8,128)S(1)} all-to-all(f32[8,128,128]{2,1,0:T(8,128)S(1)} %shard_map.28), channel_id=1, replica_groups=mesh['row'=8,'pair'=64] {'row'}, dimensions={0} | all-to-all | bytes 1048576 | tf_op jit(solution)/shard_map/all_to_all | solution.py:284
  20.3 0.0 copy-done.1
  20.3 2.8 %shard_map.29 = (f32[2048,128]{1,0:T(8,128)S(1)}, f32[256,128]{1,0:T(8,128)S(1)}) custom-call(s32[128]{0:T(128)S(1)} %copy-done.1, f32[8,128,128]{2,1,0:T(8,128)S(1)} %all_to_all.10.g_ref, f32[2048,256]{1,0:T(8,128)S(1)} %copy-done), custom_call_target="tpu_custom_call" | custom-call | flops 402653184 | bytes 2097152 | tf_op jit(solution)/shard_map/pallas_call | solution.py:181
  23.2 2.5 %collective-permute-start = (f32[2048,128]{1,0:T(8,128)S(1)}, f32[2048,128]{1,0:T(8,128)S(1)}, u32[]{:S(2)}, u32[]{:S(2)}) collective-permute-start(f32[2048,128]{1,0:T(8,128)S(1)} %get-tuple-element.10.x1_ref), channel_id=1, source_target_pairs={{3,1},{5,3},{7,5},{9,7},{11,9},{13,11},{15,13},{17,15},{19,17},{21... | collective-permute-start | bytes 3145736 | tf_op jit(solution)/shard_map/ppermute | solution.py:286
  25.7 0.7 shard_map.30.x_ref
  26.4 22.2 %collective-permute-done.y_ref.y2_ref = f32[2048,128]{1,0:T(8,128)S(1)} collective-permute-done((f32[2048,128]{1,0:T(8,128)S(1)}, f32[2048,128]{1,0:T(8,128)S(1)}, u32[]{:S(2)}, u32[]{:S(2)}) %collective-permute-start) | collective-permute-done | bytes 1048608 | tf_op jit(solution)/shard_map/ppermute | solution.py:286
  48.6 0.5 shard_map.31
  49.1 2.7 %collective-permute-start.4 = (f32[2048,128]{1,0:T(8,128)S(1)}, f32[2048,128]{1,0:T(8,128)S(1)}, u32[]{:S(2)}, u32[]{:S(2)}) collective-permute-start(f32[2048,128]{1,0:T(8,128)S(1)} %get-tuple-element.12.x2_ref), channel_id=1, source_target_pairs={{1,3},{3,5},{5,7},{7,9},{9,11},{11,13},{13,15},{15,17},{17,19},{19... | collective-permute-start | bytes 3145736 | tf_op jit(solution)/shard_map/ppermute | solution.py:289
  51.8 9.3 %all_to_all.11.refs_0_ = f32[4,128,128]{2,1,0:T(8,128)S(1)} all-to-all(f32[4,128,128]{2,1,0:T(8,128)S(1)} %get-tuple-element.11), channel_id=1, replica_groups={{0,64,128,192},{256,320,384,448},{1,65,129,193},{257,321,385,449},{2,66..., dimensions={0} | all-to-all | bytes 524288 | tf_op jit(solution)/shard_map/all_to_all | solution.py:290
  61.1 3.5 %collective-permute-start.3 = (f32[1,128,128]{2,1,0:T(8,128)S(1)}, f32[1,128,128]{2,1,0:T(8,128)S(1)}, u32[]{:S(2)}, u32[]{:S(2)}) collective-permute-start(f32[1,128,128]{2,1,0:T(8,128)S(1)} %shard_map.32.c_ref), channel_id=1, source_target_pairs={{0,256},{64,320},{128,384},{192,448},{256,0},{320,64},{384,128},{4... | collective-permute-start | bytes 196616 | tf_op jit(solution)/shard_map/ppermute | solution.py:293
  64.7 4.3 %collective-permute-start.2 = (f32[1,128,128]{2,1,0:T(8,128)S(1)}, f32[1,128,128]{2,1,0:T(8,128)S(1)}, u32[]{:S(2)}, u32[]{:S(2)}) collective-permute-start(f32[1,128,128]{2,1,0:T(8,128)S(1)} %shard_map.32.c_ref), channel_id=1, source_target_pairs={{1,259},{3,261},{5,263},{7,265},{9,267},{11,269},{13,271},{15,273}... | collective-permute-start | bytes 196616 | tf_op jit(solution)/shard_map/ppermute | solution.py:292
  69.0 1.9 %collective-permute-start.1 = (f32[1,128,128]{2,1,0:T(8,128)S(1)}, f32[1,128,128]{2,1,0:T(8,128)S(1)}, u32[]{:S(2)}, u32[]{:S(2)}) collective-permute-start(f32[1,128,128]{2,1,0:T(8,128)S(1)} %shard_map.32.c_ref), channel_id=1, source_target_pairs={{1,3},{3,5},{5,7},{7,9},{9,11},{11,13},{13,15},{15,17},{17,19},{19... | collective-permute-start | bytes 196616 | tf_op jit(solution)/shard_map/ppermute | solution.py:291
  70.9 0.6 collective-permute-done.3.d_ref
  71.5 1.4 %collective-permute-done.2.b_ref = f32[1,128,128]{2,1,0:T(8,128)S(1)} collective-permute-done((f32[1,128,128]{2,1,0:T(8,128)S(1)}, f32[1,128,128]{2,1,0:T(8,128)S(1)}, u32[]{:S(2)}, u32[]{:S(2)}) %collective-permute-start.2) | collective-permute-done | bytes 65568 | tf_op jit(solution)/shard_map/ppermute | solution.py:292
  72.9 6.3 %collective-permute-done.1.a_ref = f32[1,128,128]{2,1,0:T(8,128)S(1)} collective-permute-done((f32[1,128,128]{2,1,0:T(8,128)S(1)}, f32[1,128,128]{2,1,0:T(8,128)S(1)}, u32[]{:S(2)}, u32[]{:S(2)}) %collective-permute-start.1) | collective-permute-done | bytes 65568 | tf_op jit(solution)/shard_map/ppermute | solution.py:291
  79.2 0.0 collective-permute-done.4.y1_ref
  79.2 4.3 %shard_map.33 = f32[2048,256]{1,0:T(8,128)} custom-call(s32[128]{0:T(128)S(1)} %copy-done.1, f32[1,128,128]{2,1,0:T(8,128)S(1)} %collective-permute-done.1.a_ref, f32[1,128,128]{2,1,0:T(8,128)S(1)} %collective-permute-done.2.b_ref, f32[1,128,128]{2,1,0:T(8,128)S(1)} %shard_map.32.c_ref, f32[1,128,128]{2,1,0:T(8,128)S(1)} %collective-permute-done.3.d_ref, ...), custom_call_target="tpu_custom_call" | custom-call | flops 805306368 | bytes 2097152 | tf_op jit(solution)/shard_map/pallas_call | solution.py:255
  (1 shorter events, 0.0 us)
Async XLA Ops:
  0.0 1.6 %copy-start = (f32[2048,256]{1,0:T(8,128)S(1)}, f32[2048,256]{1,0:T(8,128)}, u32[]{:S(2)}) copy-start(f32[2048,256]{1,0:T(8,128)} %x_ref.5) | copy-start | bytes 6291460
  1.6 18.8 %copy-start.1 = (s32[128]{0:T(128)S(1)}, s32[128]{0:T(128)}, u32[]{:S(2)}) copy-start(s32[128]{0:T(128)} %ids_ref.3) | copy-start | bytes 1540
  23.2 25.4 %collective-permute-start = (f32[2048,128]{1,0:T(8,128)S(1)}, f32[2048,128]{1,0:T(8,128)S(1)}, u32[]{:S(2)}, u32[]{:S(2)}) collective-permute-start(f32[2048,128]{1,0:T(8,128)S(1)} %get-tuple-element.10.x1_ref), channel_id=1, source_target_pairs={{3,1},{5,3},{7,5},{9,7},{11,9},{13,11},{15,13},{17,15},{19,17},{21... | collective-permute-start | bytes 3145736 | tf_op jit(solution)/shard_map/ppermute | solution.py:286
  49.1 30.1 %collective-permute-start.4 = (f32[2048,128]{1,0:T(8,128)S(1)}, f32[2048,128]{1,0:T(8,128)S(1)}, u32[]{:S(2)}, u32[]{:S(2)}) collective-permute-start(f32[2048,128]{1,0:T(8,128)S(1)} %get-tuple-element.12.x2_ref), channel_id=1, source_target_pairs={{1,3},{3,5},{5,7},{7,9},{9,11},{11,13},{13,15},{15,17},{17,19},{19... | collective-permute-start | bytes 3145736 | tf_op jit(solution)/shard_map/ppermute | solution.py:289
  61.1 10.4 %collective-permute-start.3 = (f32[1,128,128]{2,1,0:T(8,128)S(1)}, f32[1,128,128]{2,1,0:T(8,128)S(1)}, u32[]{:S(2)}, u32[]{:S(2)}) collective-permute-start(f32[1,128,128]{2,1,0:T(8,128)S(1)} %shard_map.32.c_ref), channel_id=1, source_target_pairs={{0,256},{64,320},{128,384},{192,448},{256,0},{320,64},{384,128},{4... | collective-permute-start | bytes 196616 | tf_op jit(solution)/shard_map/ppermute | solution.py:293
  64.7 8.2 %collective-permute-start.2 = (f32[1,128,128]{2,1,0:T(8,128)S(1)}, f32[1,128,128]{2,1,0:T(8,128)S(1)}, u32[]{:S(2)}, u32[]{:S(2)}) collective-permute-start(f32[1,128,128]{2,1,0:T(8,128)S(1)} %shard_map.32.c_ref), channel_id=1, source_target_pairs={{1,259},{3,261},{5,263},{7,265},{9,267},{11,269},{13,271},{15,273}... | collective-permute-start | bytes 196616 | tf_op jit(solution)/shard_map/ppermute | solution.py:292
  69.0 10.2 %collective-permute-start.1 = (f32[1,128,128]{2,1,0:T(8,128)S(1)}, f32[1,128,128]{2,1,0:T(8,128)S(1)}, u32[]{:S(2)}, u32[]{:S(2)}) collective-permute-start(f32[1,128,128]{2,1,0:T(8,128)S(1)} %shard_map.32.c_ref), channel_id=1, source_target_pairs={{1,3},{3,5},{5,7},{7,9},{9,11},{11,13},{13,15},{15,17},{17,19},{19... | collective-permute-start | bytes 196616 | tf_op jit(solution)/shard_map/ppermute | solution.py:291

commit v5 on v4

--- a/solution.py
+++ b/solution.py
@@ -55,28 +55,28 @@
     return (wide[:, :BLK] + wide[:, BLK:]) + dot(al, b[0])
 
 
-def mm(a, b, dims=NN):
-    return mm_parts(halves(a), halves(b), dims)
-
-
 def eye():
     i = lax.broadcasted_iota(jnp.int32, (BLK, BLK), 0)
     j = lax.broadcasted_iota(jnp.int32, (BLK, BLK), 1)
     return jnp.where(i == j, 1.0, 0.0).astype(jnp.float32)
 
 
-def inverse_roots(mats):
+def inverse_roots(mats, kappas, sides):
     ident = eye()
     ys = [halves(m) for m in mats]
     fs = [1.5 * ident - 0.5 * m for m in mats]
     zs = fs
-    for _ in range(1, NS_ITERS):
+    for sweep in range(1, NS_ITERS):
         fps = [halves(f) for f in fs]
         ys = [halves(mm_parts(y, f)) for y, f in zip(ys, fps)]
         zps = [halves(z) for z in zs]
         fs = [1.5 * ident - 0.5 * mm_parts(z, y) for z, y in zip(zps, ys)]
-        zs = [mm_parts(halves(f), z) for f, z in zip(fs, zps)]
-    return [z * (5.0**-0.5) for z in zs]
+        if sweep == NS_ITERS - 1:
+            ks = [halves(mm_parts(k, z, d)) for k, z, d in zip(kappas, zps, sides)]
+        fps = [halves(f) for f in fs]
+        zs = [mm_parts(f, z) for f, z in zip(fps, zps)]
+    scale = 5.0**-0.5
+    return [z * scale for z in zs], [mm_parts(k, f) * scale for k, f in zip(ks, fps)]
 
 
 def tangent(cross, sign):
@@ -166,9 +166,9 @@
         ident = eye()
         left = (ident + mm_parts(kp, kp, NT)) / 5.0
         right = (ident + mm_parts(kp, kp, TN)) / 5.0
-        linv, rinv = inverse_roots([left, right])
-        up = jnp.concatenate([linv, mm(kappa, linv, TN)], axis=0)
-        low = jnp.concatenate([-mm(kappa, rinv), rinv], axis=0)
+        (linv, rinv), (lk, kr) = inverse_roots([left, right], [kp, kp], [TN, NN])
+        up = jnp.concatenate([linv, lk], axis=0)
+        low = jnp.concatenate([-kr, rinv], axis=0)
         w_ref[...] = jnp.where(upper_first, up, low)
         wp = halves(jnp.where(upper_first, low, up))
         for c in chunks(rows):
@@ -226,14 +226,12 @@
             cross = jnp.where(flip, crosses[k].T, crosses[k])
             kappas.append(tangent(cross, jnp.where(swaps[k], -sign, sign)))
         ident = eye()
-        rights = []
-        for kappa in kappas:
-            kp = halves(kappa)
-            rights.append((ident + mm_parts(kp, kp, TN)) / 5.0)
-        rinvs = inverse_roots(rights)
+        kps = [halves(kappa) for kappa in kappas]
+        rights = [(ident + mm_parts(kp, kp, TN)) / 5.0 for kp in kps]
+        rinvs, krs = inverse_roots(rights, kps, [NN, NN])
         wps = []
         for k in range(2):
-            other = -mm(kappas[k], rinvs[k])
+            other = -krs[k]
             w = [jnp.where(swaps[k], rinvs[k], other), jnp.where(swaps[k], other, rinvs[k])]
             wps.append(halves(jnp.concatenate(w, axis=0)))
         columns = [jnp.where(odd, 0, BLK), jnp.where(odd, BLK, 0)]
@@ -241,13 +239,11 @@
         for i, c in enumerate(chunks(rows)):
             for k, (x_ref, y_ref) in enumerate(((x1_ref, y1_ref), (x2_ref, y2_ref))):
                 z = jnp.concatenate([x_ref[c, :], y_ref[c, :]], axis=1)
-                buf_ref[k, c, :] = mm_narrow(z, wps[k])
                 column = pl.multiple_of(columns[k], BLK)
-                copy = pltpu.make_async_copy(
-                    buf_ref.at[k, c, :], o_ref.at[c, pl.ds(column, BLK)], sems.at[k, i]
-                )
-                copy.start()
-                copies.append(copy)
+                buf_ref[c, pl.ds(column, BLK)] = mm_narrow(z, wps[k])
+            copy = pltpu.make_async_copy(buf_ref.at[c, :], o_ref.at[c, :], sems.at[i])
+            copy.start()
+            copies.append(copy)
         for copy in copies:
             copy.wait()
 
@@ -259,8 +255,8 @@
         ANY,
         rows * BLK * BLK * 24,
         scratch=[
-            pltpu.VMEM((2, rows, BLK), jnp.float32),
-            pltpu.SemaphoreType.DMA((2, steps)),
+            pltpu.VMEM((rows, 2 * BLK), jnp.float32),
+            pltpu.SemaphoreType.DMA((steps,)),
         ],
     )(*operands)
 

time: 83.8 us -> 83.5 us (level)
  no operation moved by 1% of the time
where the time goes in v5:
time: 83.5 us; the launch traced here: 83.2 us
  waiting for transfers between devices  30.4 us (36%)
  blocking collectives  27.6 us (33%)
  starting transfers between devices  15 us (18%)
  Pallas kernels  8.54 us (10%)
  local copies, waits for them, and re-layouts  1.59 us (2%)
    ppermute x1, waiting for transfers between devices, per_device(): first = lax.ppermute(two, 'pair', back)  22.2 us
    all_to_all x1, blocking collectives, per_device(): gathered = exchange(cross_of_panel(panel, count))  18.3 us
    all_to_all x1, blocking collectives, per_device(): part = total_of([exchange(partial, axis_index_groups=near)], 1)  9.3 us
    ppermute x1, waiting for transfers between devices, per_device(): back_near = lax.ppermute(part, 'pair', there)  6.29 us
    ppermute x1, starting transfers between devices, per_device(): back_far = lax.ppermute(part, ('row', 'pair'), back_across)  4.33 us
    pallas_call x1, Pallas kernels, rotate_pairs(): call(kernel, jax.ShapeDtypeStruct((rows, 2 * BLK), jnp.float32), [SMEM] +...  4.14 us
    ppermute x1, starting transfers between devices, per_device(): other = lax.ppermute(part, 'row', across)  3.52 us
    ppermute x1, starting transfers between devices, per_device(): second = lax.ppermute(one, 'pair', there)  2.73 us
  transfers between devices with their start and end apart: 5, of which 4 were waited for; matrix products, arithmetic and copies ran while one was open for 0% of the time, Pallas kernels for 1%

profile of v5, /device:TPU:96, one launch (start us, length us, event | category | flops | bytes accessed | tf_op | source)
XLA Modules:
  0.0 83.2 jit_solution(16879681784227102963)
XLA Ops:
  0.0 0.0 copy-start
  0.0 1.6 %copy-done = f32[2048,256]{1,0:T(8,128)S(1)} copy-done((f32[2048,256]{1,0:T(8,128)S(1)}, f32[2048,256]{1,0:T(8,128)}, u32[]{:S(2)}) %copy-start) | copy-done | bytes 2097176
  1.6 0.0 copy-start.1
  1.6 0.5 shard_map.28
  2.1 18.3 %all_to_all.10.g_ref = f32[8,128,128]{2,1,0:T(8,128)S(1)} all-to-all(f32[8,128,128]{2,1,0:T(8,128)S(1)} %shard_map.28), channel_id=1, replica_groups=mesh['row'=8,'pair'=64] {'row'}, dimensions={0} | all-to-all | bytes 1048576 | tf_op jit(solution)/shard_map/all_to_all | solution.py:280
  20.3 0.0 copy-done.1
  20.3 2.7 %shard_map.29 = (f32[2048,128]{1,0:T(8,128)S(1)}, f32[256,128]{1,0:T(8,128)S(1)}) custom-call(s32[128]{0:T(128)S(1)} %copy-done.1, f32[8,128,128]{2,1,0:T(8,128)S(1)} %all_to_all.10.g_ref, f32[2048,256]{1,0:T(8,128)S(1)} %copy-done), custom_call_target="tpu_custom_call" | custom-call | flops 402653184 | bytes 2097152 | tf_op jit(solution)/shard_map/pallas_call | solution.py:181
  23.1 2.5 %collective-permute-start = (f32[2048,128]{1,0:T(8,128)S(1)}, f32[2048,128]{1,0:T(8,128)S(1)}, u32[]{:S(2)}, u32[]{:S(2)}) collective-permute-start(f32[2048,128]{1,0:T(8,128)S(1)} %get-tuple-element.10.x1_ref), channel_id=1, source_target_pairs={{3,1},{5,3},{7,5},{9,7},{11,9},{13,11},{15,13},{17,15},{19,17},{21... | collective-permute-start | bytes 3145736 | tf_op jit(solution)/shard_map/ppermute | solution.py:282
  25.6 0.7 shard_map.30.x_ref
  26.3 22.2 %collective-permute-done.y_ref.y2_ref = f32[2048,128]{1,0:T(8,128)S(1)} collective-permute-done((f32[2048,128]{1,0:T(8,128)S(1)}, f32[2048,128]{1,0:T(8,128)S(1)}, u32[]{:S(2)}, u32[]{:S(2)}) %collective-permute-start) | collective-permute-done | bytes 1048608 | tf_op jit(solution)/shard_map/ppermute | solution.py:282
  48.5 0.5 shard_map.31
  49.0 2.7 %collective-permute-start.4 = (f32[2048,128]{1,0:T(8,128)S(1)}, f32[2048,128]{1,0:T(8,128)S(1)}, u32[]{:S(2)}, u32[]{:S(2)}) collective-permute-start(f32[2048,128]{1,0:T(8,128)S(1)} %get-tuple-element.12.x2_ref), channel_id=1, source_target_pairs={{1,3},{3,5},{5,7},{7,9},{9,11},{11,13},{13,15},{15,17},{17,19},{19... | collective-permute-start | bytes 3145736 | tf_op jit(solution)/shard_map/ppermute | solution.py:285
  51.7 9.3 %all_to_all.11.refs_0_ = f32[4,128,128]{2,1,0:T(8,128)S(1)} all-to-all(f32[4,128,128]{2,1,0:T(8,128)S(1)} %get-tuple-element.11), channel_id=1, replica_groups={{0,64,128,192},{256,320,384,448},{1,65,129,193},{257,321,385,449},{2,66..., dimensions={0} | all-to-all | bytes 524288 | tf_op jit(solution)/shard_map/all_to_all | solution.py:286
  61.0 3.5 %collective-permute-start.3 = (f32[1,128,128]{2,1,0:T(8,128)S(1)}, f32[1,128,128]{2,1,0:T(8,128)S(1)}, u32[]{:S(2)}, u32[]{:S(2)}) collective-permute-start(f32[1,128,128]{2,1,0:T(8,128)S(1)} %shard_map.32.c_ref), channel_id=1, source_target_pairs={{0,256},{64,320},{128,384},{192,448},{256,0},{320,64},{384,128},{4... | collective-permute-start | bytes 196616 | tf_op jit(solution)/shard_map/ppermute | solution.py:289
  64.5 4.3 %collective-permute-start.2 = (f32[1,128,128]{2,1,0:T(8,128)S(1)}, f32[1,128,128]{2,1,0:T(8,128)S(1)}, u32[]{:S(2)}, u32[]{:S(2)}) collective-permute-start(f32[1,128,128]{2,1,0:T(8,128)S(1)} %shard_map.32.c_ref), channel_id=1, source_target_pairs={{1,259},{3,261},{5,263},{7,265},{9,267},{11,269},{13,271},{15,273}... | collective-permute-start | bytes 196616 | tf_op jit(solution)/shard_map/ppermute | solution.py:288
  68.9 1.9 %collective-permute-start.1 = (f32[1,128,128]{2,1,0:T(8,128)S(1)}, f32[1,128,128]{2,1,0:T(8,128)S(1)}, u32[]{:S(2)}, u32[]{:S(2)}) collective-permute-start(f32[1,128,128]{2,1,0:T(8,128)S(1)} %shard_map.32.c_ref), channel_id=1, source_target_pairs={{1,3},{3,5},{5,7},{7,9},{9,11},{11,13},{13,15},{15,17},{17,19},{19... | collective-permute-start | bytes 196616 | tf_op jit(solution)/shard_map/ppermute | solution.py:287
  70.8 0.6 collective-permute-done.3.d_ref
  71.4 1.4 %collective-permute-done.2.b_ref = f32[1,128,128]{2,1,0:T(8,128)S(1)} collective-permute-done((f32[1,128,128]{2,1,0:T(8,128)S(1)}, f32[1,128,128]{2,1,0:T(8,128)S(1)}, u32[]{:S(2)}, u32[]{:S(2)}) %collective-permute-start.2) | collective-permute-done | bytes 65568 | tf_op jit(solution)/shard_map/ppermute | solution.py:288
  72.8 6.3 %collective-permute-done.1.a_ref = f32[1,128,128]{2,1,0:T(8,128)S(1)} collective-permute-done((f32[1,128,128]{2,1,0:T(8,128)S(1)}, f32[1,128,128]{2,1,0:T(8,128)S(1)}, u32[]{:S(2)}, u32[]{:S(2)}) %collective-permute-start.1) | collective-permute-done | bytes 65568 | tf_op jit(solution)/shard_map/ppermute | solution.py:287
  79.1 0.0 collective-permute-done.4.y1_ref
  79.1 4.1 %shard_map.33 = f32[2048,256]{1,0:T(8,128)} custom-call(s32[128]{0:T(128)S(1)} %copy-done.1, f32[1,128,128]{2,1,0:T(8,128)S(1)} %collective-permute-done.1.a_ref, f32[1,128,128]{2,1,0:T(8,128)S(1)} %collective-permute-done.2.b_ref, f32[1,128,128]{2,1,0:T(8,128)S(1)} %shard_map.32.c_ref, f32[1,128,128]{2,1,0:T(8,128)S(1)} %collective-permute-done.3.d_ref, ...), custom_call_target="tpu_custom_call" | custom-call | flops 805306368 | bytes 2097152 | tf_op jit(solution)/shard_map/pallas_call | solution.py:251
  (1 shorter events, 0.0 us)
Async XLA Ops:
  0.0 1.6 %copy-start = (f32[2048,256]{1,0:T(8,128)S(1)}, f32[2048,256]{1,0:T(8,128)}, u32[]{:S(2)}) copy-start(f32[2048,256]{1,0:T(8,128)} %x_ref.5) | copy-start | bytes 6291460
  1.6 18.8 %copy-start.1 = (s32[128]{0:T(128)S(1)}, s32[128]{0:T(128)}, u32[]{:S(2)}) copy-start(s32[128]{0:T(128)} %ids_ref.3) | copy-start | bytes 1540
  23.1 25.4 %collective-permute-start = (f32[2048,128]{1,0:T(8,128)S(1)}, f32[2048,128]{1,0:T(8,128)S(1)}, u32[]{:S(2)}, u32[]{:S(2)}) collective-permute-start(f32[2048,128]{1,0:T(8,128)S(1)} %get-tuple-element.10.x1_ref), channel_id=1, source_target_pairs={{3,1},{5,3},{7,5},{9,7},{11,9},{13,11},{15,13},{17,15},{19,17},{21... | collective-permute-start | bytes 3145736 | tf_op jit(solution)/shard_map/ppermute | solution.py:282
  49.0 30.1 %collective-permute-start.4 = (f32[2048,128]{1,0:T(8,128)S(1)}, f32[2048,128]{1,0:T(8,128)S(1)}, u32[]{:S(2)}, u32[]{:S(2)}) collective-permute-start(f32[2048,128]{1,0:T(8,128)S(1)} %get-tuple-element.12.x2_ref), channel_id=1, source_target_pairs={{1,3},{3,5},{5,7},{7,9},{9,11},{11,13},{13,15},{15,17},{17,19},{19... | collective-permute-start | bytes 3145736 | tf_op jit(solution)/shard_map/ppermute | solution.py:285
  61.0 10.4 %collective-permute-start.3 = (f32[1,128,128]{2,1,0:T(8,128)S(1)}, f32[1,128,128]{2,1,0:T(8,128)S(1)}, u32[]{:S(2)}, u32[]{:S(2)}) collective-permute-start(f32[1,128,128]{2,1,0:T(8,128)S(1)} %shard_map.32.c_ref), channel_id=1, source_target_pairs={{0,256},{64,320},{128,384},{192,448},{256,0},{320,64},{384,128},{4... | collective-permute-start | bytes 196616 | tf_op jit(solution)/shard_map/ppermute | solution.py:289
  64.5 8.2 %collective-permute-start.2 = (f32[1,128,128]{2,1,0:T(8,128)S(1)}, f32[1,128,128]{2,1,0:T(8,128)S(1)}, u32[]{:S(2)}, u32[]{:S(2)}) collective-permute-start(f32[1,128,128]{2,1,0:T(8,128)S(1)} %shard_map.32.c_ref), channel_id=1, source_target_pairs={{1,259},{3,261},{5,263},{7,265},{9,267},{11,269},{13,271},{15,273}... | collective-permute-start | bytes 196616 | tf_op jit(solution)/shard_map/ppermute | solution.py:288
  68.9 10.2 %collective-permute-start.1 = (f32[1,128,128]{2,1,0:T(8,128)S(1)}, f32[1,128,128]{2,1,0:T(8,128)S(1)}, u32[]{:S(2)}, u32[]{:S(2)}) collective-permute-start(f32[1,128,128]{2,1,0:T(8,128)S(1)} %shard_map.32.c_ref), channel_id=1, source_target_pairs={{1,3},{3,5},{5,7},{7,9},{9,11},{11,13},{13,15},{15,17},{17,19},{19... | collective-permute-start | bytes 196616 | tf_op jit(solution)/shard_map/ppermute | solution.py:287
